TPU v7x, 256 devices: a whole 4x4x8 slice. The times are simulated.
256 devices in a mesh: row: 32 (over x_lo, z, core), col: 8 (over x_hi, y).
Axes of the slice: x: 4 (x_hi: 2, x_lo: 2; x = x_hi * 2 + x_lo), y: 4, z: 8, core: 2. Of those that a mesh axis runs over, the one named last changes fastest.
Arguments:
- embeddings: bfloat16 [131072, 768], P(('row', 'col')), may hold values from -7.5 to 7.5
- block_cluster: int32 [512], replicated, may hold values from 0 to 127, never falling along the last dimension, each value on 1 to 8 neighbouring positions
- partner_shift: int32 [131072], P(('row', 'col')), may hold values from 1 to 255
Outputs:
- item_loss: float32 [131072], P(('row', 'col'))
- embedding_grad: float32 [131072, 768], P(('row', 'col'))
Inputs may be any that keep to these rules, and one draw needn't show every extreme that they name: block_cluster never falls along the blocks; each value is held by 1 to 8 consecutive blocks, and some value by exactly 8.
All inputs are finite; a program needn't handle non-finite values.
Results may differ from a plain program's by a relative error of at most 0.0018.
Values may be sent and summed in bfloat16 or wider, within the bound.
No kernel may reach another device: no remote copies, remote signals or barrier semaphores. Data moves between devices by JAX's collectives and lax.ppermute only.
A program may use at most 128 MiB of HBM per device.

v0:
```python
import jax
import jax.numpy as jnp
from jax import lax
from jax.sharding import PartitionSpec as P

BLOCK = 256
REACH = 4


NEG = -1e30


def shifted(value, axis, steps):
    count = lax.axis_size(axis)
    leading, last = (max(0, -steps), min(count, count - steps))
    return lax.ppermute(value, axis, [(source, source + steps) for source in range(leading, last)])


def fetch_ahead(values, offset):
    return shifted(values, ("row", "col"), -offset)


def fetch_behind(values, offset):
    return shifted(values, ("row", "col"), offset)


def lse_ahead(values, offset):
    return shifted(values, ("row", "col"), -offset)


def lse_behind(values, offset):
    return shifted(values, ("row", "col"), offset)


def pair_scores(left, right, scale):
    return (
        lax.dot_general(left, right, (((1,), (1,)), ((), ())), preferred_element_type=jnp.float32)
        * scale
    )


def row_stats(scores, live):
    masked = jnp.where(live, scores, NEG)
    top = jnp.max(masked, axis=1)
    total = jnp.sum(jnp.where(live, jnp.exp(masked - top[:, None]), 0.0), axis=1)
    return (top, total)


def merge_stats(first, second):
    top = jnp.maximum(first[0], second[0])
    total = first[1] * jnp.exp(first[0] - top) + second[1] * jnp.exp(second[0] - top)
    return (top, total)


def tile_weights(scores, live, lse, far_lse):
    rowwise = jnp.exp(jnp.where(live, scores - lse[:, None], NEG))
    colwise = jnp.exp(jnp.where(live, scores - far_lse[None, :], NEG))
    return (rowwise + colwise).astype(jnp.bfloat16)


def shards(embeddings, block_cluster, partner_shift):
    rows = embeddings.shape[0]
    width = embeddings.shape[1]
    scale = width ** (-0.5)
    blocks_here = rows // BLOCK
    device = lax.axis_index(("row", "col"))
    margin = jnp.full((REACH * blocks_here,), -1, jnp.int32)
    beyond = jnp.full((REACH * blocks_here,), -2, jnp.int32)
    padded = jnp.concatenate([margin, block_cluster, beyond])
    start_block = device * blocks_here
    nearby = lax.dynamic_slice_in_dim(padded, start_block, (2 * REACH + 1) * blocks_here)

    def clusters_at(offset):
        begin = (REACH + offset) * blocks_here
        return jnp.repeat(nearby[begin : begin + blocks_here], BLOCK)

    mine = clusters_at(0)

    def live_at(offset):
        return mine[:, None] == clusters_at(offset)[None, :]

    position = jnp.arange(rows, dtype=jnp.int32)
    diagonal = position[:, None] == position[None, :]
    live_self = live_at(0) & jnp.logical_not(diagonal)
    within = position % BLOCK
    partner = position - within + (within + partner_shift) % BLOCK
    positive = position[None, :] == partner[:, None]
    self_scores = pair_scores(embeddings, embeddings, scale)
    stats = row_stats(self_scores, live_self)
    ahead_tiles = []
    behind_tiles = []
    for offset in range(1, REACH + 1):
        ahead = fetch_ahead(embeddings, offset)
        live = live_at(offset)
        scores = pair_scores(embeddings, ahead, scale)
        stats = merge_stats(stats, row_stats(scores, live))
        ahead_tiles.append((ahead, scores, live))
        behind = fetch_behind(embeddings, offset)
        live_back = live_at(-offset)
        scores_back = pair_scores(embeddings, behind, scale)
        stats = merge_stats(stats, row_stats(scores_back, live_back))
        behind_tiles.append((behind, scores_back, live_back))
    lse = stats[0] + jnp.log(stats[1])
    item_loss = lse - jnp.sum(jnp.where(positive, self_scores, 0.0), axis=1)
    self_terms = jnp.exp(jnp.where(live_self, self_scores - lse[:, None], NEG)) - positive.astype(
        jnp.float32
    )
    self_weights = (self_terms + self_terms.T).astype(jnp.bfloat16)
    grad = jnp.dot(self_weights, embeddings, preferred_element_type=jnp.float32) * scale
    for offset in range(1, REACH + 1):
        ahead, scores, live = ahead_tiles[offset - 1]
        far_lse = lse_ahead(lse, offset)
        weights = tile_weights(scores, live, lse, far_lse)
        grad = grad + jnp.dot(weights, ahead, preferred_element_type=jnp.float32) * scale
        behind, scores_back, live_back = behind_tiles[offset - 1]
        back_lse = lse_behind(lse, offset)
        weights_back = tile_weights(scores_back, live_back, lse, back_lse)
        grad = grad + jnp.dot(weights_back, behind, preferred_element_type=jnp.float32) * scale
    return (item_loss, grad)


def solution(mesh):
    in_specs = (P(("row", "col"), None), P(), P(("row", "col")))
    out_specs = (P(("row", "col")), P(("row", "col"), None))
    return jax.shard_map(shards, mesh=mesh, in_specs=in_specs, out_specs=out_specs, check_vma=False)
```

profile of v0, /device:TPU:103, one launch (start us, length us, event | category | flops | bytes accessed | tf_op | source)
XLA Modules:
  0.0 207.3 jit_solution(14182472613452262768)
XLA Ops:
  0.6 5.5 %collective-permute-start = (bf16[512,768]{1,0:T(8,128)(2,1)}, bf16[512,768]{1,0:T(8,128)(2,1)}, u32[]{:S(2)}, u32[]{:S(2)}) collective-permute-start(bf16[512,768]{1,0:T(8,128)(2,1)} %param.3), channel_id=1, source_target_pairs={{1,0},{2,1},{3,2},{4,3},{5,4},{6,5},{7,6},{8,7},{9,8},{10,9},{11,1... | collective-permute-start | bytes 2359304 | tf_op jit(solution)/shard_map/ppermute | solution.py:16
  6.1 2.3 %collective-permute-start.2 = (bf16[512,768]{1,0:T(8,128)(2,1)}, bf16[512,768]{1,0:T(8,128)(2,1)}, u32[]{:S(2)}, u32[]{:S(2)}) collective-permute-start(bf16[512,768]{1,0:T(8,128)(2,1)} %param.3), channel_id=1, source_target_pairs={{2,0},{3,1},{4,2},{5,3},{6,4},{7,5},{8,6},{9,7},{10,8},{11,9},{12,... | collective-permute-start | bytes 2359304 | tf_op jit(solution)/shard_map/ppermute | solution.py:16
  8.4 4.5 %collective-permute-start.3 = (bf16[512,768]{1,0:T(8,128)(2,1)}, bf16[512,768]{1,0:T(8,128)(2,1)}, u32[]{:S(2)}, u32[]{:S(2)}) collective-permute-start(bf16[512,768]{1,0:T(8,128)(2,1)} %param.3), channel_id=1, source_target_pairs={{0,2},{1,3},{2,4},{3,5},{4,6},{5,7},{6,8},{7,9},{8,10},{9,11},{10,... | collective-permute-start | bytes 2359304 | tf_op jit(solution)/shard_map/ppermute | solution.py:16
  12.9 2.4 %collective-permute-start.4 = (bf16[512,768]{1,0:T(8,128)(2,1)}, bf16[512,768]{1,0:T(8,128)(2,1)}, u32[]{:S(2)}, u32[]{:S(2)}) collective-permute-start(bf16[512,768]{1,0:T(8,128)(2,1)} %param.3), channel_id=1, source_target_pairs={{3,0},{4,1},{5,2},{6,3},{7,4},{8,5},{9,6},{10,7},{11,8},{12,9},{13... | collective-permute-start | bytes 2359304 | tf_op jit(solution)/shard_map/ppermute | solution.py:16
  15.3 5.9 %collective-permute-start.5 = (bf16[512,768]{1,0:T(8,128)(2,1)}, bf16[512,768]{1,0:T(8,128)(2,1)}, u32[]{:S(2)}, u32[]{:S(2)}) collective-permute-start(bf16[512,768]{1,0:T(8,128)(2,1)} %param.3), channel_id=1, source_target_pairs={{0,3},{1,4},{2,5},{3,6},{4,7},{5,8},{6,9},{7,10},{8,11},{9,12},{10... | collective-permute-start | bytes 2359304 | tf_op jit(solution)/shard_map/ppermute | solution.py:16
  24.3 37.4 %collective-permute-done.2 = bf16[512,768]{1,0:T(8,128)(2,1)} collective-permute-done((bf16[512,768]{1,0:T(8,128)(2,1)}, bf16[512,768]{1,0:T(8,128)(2,1)}, u32[]{:S(2)}, u32[]{:S(2)}) %collective-permute-start.2) | collective-permute-done | bytes 786464 | tf_op jit(solution)/shard_map/ppermute | solution.py:16
  61.7 5.4 %collective-permute-start.6 = (bf16[512,768]{1,0:T(8,128)(2,1)S(1)}, bf16[512,768]{1,0:T(8,128)(2,1)S(1)}, u32[]{:S(2)}, u32[]{:S(2)}) collective-permute-start(bf16[512,768]{1,0:T(8,128)(2,1)S(1)} %copy-done), channel_id=1, source_target_pairs={{4,0},{5,1},{6,2},{7,3},{8,4},{9,5},{10,6},{11,7},{12,8},{13,9},{1... | collective-permute-start | bytes 2359304 | tf_op jit(solution)/shard_map/ppermute | solution.py:16
  68.9 4.8 %collective-permute-start.7 = (bf16[512,768]{1,0:T(8,128)(2,1)S(1)}, bf16[512,768]{1,0:T(8,128)(2,1)S(1)}, u32[]{:S(2)}, u32[]{:S(2)}) collective-permute-start(bf16[512,768]{1,0:T(8,128)(2,1)S(1)} %copy-done), channel_id=1, source_target_pairs={{0,4},{1,5},{2,6},{3,7},{4,8},{5,9},{6,10},{7,11},{8,12},{9,13},{1... | collective-permute-start | bytes 2359304 | tf_op jit(solution)/shard_map/ppermute | solution.py:16
  75.4 22.4 %collective-permute-start.1 = (bf16[512,768]{1,0:T(8,128)(2,1)S(1)}, bf16[512,768]{1,0:T(8,128)(2,1)S(1)}, u32[]{:S(2)}, u32[]{:S(2)}) collective-permute-start(bf16[512,768]{1,0:T(8,128)(2,1)S(1)} %copy-done), channel_id=1, source_target_pairs={{0,1},{1,2},{2,3},{3,4},{4,5},{5,6},{6,7},{7,8},{8,9},{9,10},{10,1... | collective-permute-start | bytes 2359304 | tf_op jit(solution)/shard_map/ppermute | solution.py:16
  99.6 2.1 %convolution_multiply_fusion.3 = f32[512,512]{1,0:T(8,128)S(1)} fusion(bf16[512,768]{1,0:T(8,128)(2,1)S(1)} %copy-done, bf16[512,768]{1,0:T(8,128)(2,1)} %collective-permute-done.4), kind=kOutput, calls=%fused_computation.36 | convolution fusion | flops 402915328 | bytes 2621440 | tf_op jit(solution)/shard_map/dot_general | solution.py:37
  101.8 2.1 %convolution_multiply_fusion.2 = f32[512,512]{1,0:T(8,128)S(1)} fusion(bf16[512,768]{1,0:T(8,128)(2,1)S(1)} %copy-done, bf16[512,768]{1,0:T(8,128)(2,1)} %collective-permute-done.5), kind=kOutput, calls=%fused_computation.35 | convolution fusion | flops 402915328 | bytes 2621440 | tf_op jit(solution)/shard_map/dot_general | solution.py:37
  105.3 3.7 %collective-permute-done.7 = bf16[512,768]{1,0:T(8,128)(2,1)S(1)} collective-permute-done((bf16[512,768]{1,0:T(8,128)(2,1)S(1)}, bf16[512,768]{1,0:T(8,128)(2,1)S(1)}, u32[]{:S(2)}, u32[]{:S(2)}) %collective-permute-start.7) | collective-permute-done | bytes 786464 | tf_op jit(solution)/shard_map/ppermute | solution.py:16
  109.5 29.8 %collective-permute-done.1 = bf16[512,768]{1,0:T(8,128)(2,1)S(1)} collective-permute-done((bf16[512,768]{1,0:T(8,128)(2,1)S(1)}, bf16[512,768]{1,0:T(8,128)(2,1)S(1)}, u32[]{:S(2)}, u32[]{:S(2)}) %collective-permute-start.1) | collective-permute-done | bytes 786464 | tf_op jit(solution)/shard_map/ppermute | solution.py:16
  141.6 2.1 %fusion.5 = (f32[512]{0:T(512)S(1)}, f32[512]{0:T(512)S(1)}, f32[512]{0:T(512)S(1)}, f32[512]{0:T(512)S(1)}, f32[512]{0:T(512)S(1)}, /*index=5*/f32[512]{0:T(512)S(1)}) fusion(f32[512,512]{1,0:T(8,128)S(1)} %get-tuple-element.32, f32[512]{0:T(512)S(1)} %get-tuple-element.4, s32[512]{0:T(512)S(1)} %bitcast.83, s32[512]{0:T(512)S(1)} %bitcast.69, ...), kind=kLoop, calls=%fused_computation.47 | loop fusion | flops 7861248 | bytes 6330368 | tf_op jit(solution)/shard_map/reduce_sum | solution.py:45
  148.2 5.8 %collective-permute-start.12 = (f32[512]{0:T(512)S(1)}, f32[512]{0:T(512)S(1)}, u32[]{:S(2)}, u32[]{:S(2)}) collective-permute-start(f32[512]{0:T(512)S(1)} %get-tuple-element.20), channel_id=1, source_target_pairs={{3,0},{4,1},{5,2},{6,3},{7,4},{8,5},{9,6},{10,7},{11,8},{12,9},{13... | collective-permute-start | bytes 6152 | tf_op jit(solution)/shard_map/ppermute | solution.py:16
  155.9 7.3 %collective-permute-start.10 = (f32[512]{0:T(512)S(1)}, f32[512]{0:T(512)S(1)}, u32[]{:S(2)}, u32[]{:S(2)}) collective-permute-start(f32[512]{0:T(512)S(1)} %get-tuple-element.20), channel_id=1, source_target_pairs={{2,0},{3,1},{4,2},{5,3},{6,4},{7,5},{8,6},{9,7},{10,8},{11,9},{12,... | collective-permute-start | bytes 6152 | tf_op jit(solution)/shard_map/ppermute | solution.py:16
  165.9 2.7 %fusion.58 = f32[512,768]{1,0:T(8,128)S(1)} fusion(bf16[512,768]{1,0:T(8,128)(2,1)S(1)} %copy-done, f32[512,512]{0,1:T(8,128)} %broadcast_subtract_fusion, f32[512,512]{1,0:T(8,128)S(1)} %copy.17, s32[512]{0:T(512)S(1)} %fusion.126, s32[512]{0:T(512)S(1)} %bitcast.70), kind=kOutput, calls=%fused_computation.107 | convolution fusion | flops 407371776 | bytes 4460544 | tf_op jit(solution)/shard_map/dot_general | solution.py:109
  168.6 4.7 %collective-permute-start.9 = (f32[512]{0:T(512)S(1)}, f32[512]{0:T(512)S(1)}, u32[]{:S(2)}, u32[]{:S(2)}) collective-permute-start(f32[512]{0:T(512)S(1)} %get-tuple-element.20), channel_id=1, source_target_pairs={{0,1},{1,2},{2,3},{3,4},{4,5},{5,6},{6,7},{7,8},{8,9},{9,10},{10,1... | collective-permute-start | bytes 6152 | tf_op jit(solution)/shard_map/ppermute | solution.py:16
  174.3 4.4 %collective-permute-start.8 = (f32[512]{0:T(512)S(1)}, f32[512]{0:T(512)S(1)}, u32[]{:S(2)}, u32[]{:S(2)}) collective-permute-start(f32[512]{0:T(512)S(1)} %get-tuple-element.20), channel_id=1, source_target_pairs={{1,0},{2,1},{3,2},{4,3},{5,4},{6,5},{7,6},{8,7},{9,8},{10,9},{11,1... | collective-permute-start | bytes 6152 | tf_op jit(solution)/shard_map/ppermute | solution.py:16
  178.7 2.0 fusion.66
  180.7 14.7 %collective-permute-start.15 = (f32[512]{0:T(512)S(1)}, f32[512]{0:T(512)S(1)}, u32[]{:S(2)}, u32[]{:S(2)}) collective-permute-start(f32[512]{0:T(512)S(1)} %get-tuple-element.20), channel_id=1, source_target_pairs={{0,4},{1,5},{2,6},{3,7},{4,8},{5,9},{6,10},{7,11},{8,12},{9,13},{1... | collective-permute-start | bytes 6152 | tf_op jit(solution)/shard_map/ppermute | solution.py:16
  197.5 2.1 %fusion.70 = f32[512,768]{1,0:T(8,128)S(1)} fusion(bf16[512,768]{1,0:T(8,128)(2,1)} %collective-permute-done.3, f32[512,512]{1,0:T(8,128)S(1)} %copy-done.10, f32[512]{0:T(512)S(1)} %collective-permute-done.11, f32[512]{0:T(512)S(1)} %get-tuple-element.20, s32[512]{0:T(512)S(1)} %bitcast.99, s32[512]{0:T(512)S(1)} %bitcast.74), kind=kOutput, calls=%fused_computation.112 | convolution fusion | flops 404488192 | bytes 3416064 | tf_op jit(solution)/shard_map/dot_general | solution.py:118
  199.6 2.1 %fusion.72 = f32[512,768]{1,0:T(8,128)S(1)} fusion(bf16[512,768]{1,0:T(8,128)(2,1)} %collective-permute-done.2, f32[512,512]{1,0:T(8,128)S(1)} %copy-done.2, f32[512]{0:T(512)S(1)} %collective-permute-done.10, f32[512]{0:T(512)S(1)} %get-tuple-element.20, s32[512]{0:T(512)S(1)} %bitcast.87, s32[512]{0:T(512)S(1)} %bitcast.75), kind=kOutput, calls=%fused_computation.113 | convolution fusion | flops 404488192 | bytes 3416064 | tf_op jit(solution)/shard_map/dot_general | solution.py:114
  205.0 2.3 %add_multiply_fusion = f32[512,768]{1,0:T(8,128)} fusion(f32[512,768]{1,0:T(8,128)S(1)} %fusion.64, f32[512,768]{1,0:T(8,128)S(1)} %fusion.66, f32[512,768]{1,0:T(8,128)S(1)} %fusion.68, f32[512,768]{1,0:T(8,128)S(1)} %fusion.70, f32[512,768]{1,0:T(8,128)S(1)} %fusion.72, f32[512,768]{1,0:T(8,128)S(1)} %fusion.74, f32[512,768]{1,0:T(8,128)S(1)} %fusion.58, ...), kind=kOutput, calls=%fused_computation.32 | convolution fusion | flops 408027136 | bytes 15998976 | tf_op jit(solution)/shard_map/dot_general | solution.py:118
  (103 shorter events, 27.5 us)
Async XLA Ops:
  0.6 74.8 %collective-permute-start = (bf16[512,768]{1,0:T(8,128)(2,1)}, bf16[512,768]{1,0:T(8,128)(2,1)}, u32[]{:S(2)}, u32[]{:S(2)}) collective-permute-start(bf16[512,768]{1,0:T(8,128)(2,1)} %param.3), channel_id=1, source_target_pairs={{1,0},{2,1},{3,2},{4,3},{5,4},{6,5},{7,6},{8,7},{9,8},{10,9},{11,1... | collective-permute-start | bytes 2359304 | tf_op jit(solution)/shard_map/ppermute | solution.py:16
  6.1 55.6 %collective-permute-start.2 = (bf16[512,768]{1,0:T(8,128)(2,1)}, bf16[512,768]{1,0:T(8,128)(2,1)}, u32[]{:S(2)}, u32[]{:S(2)}) collective-permute-start(bf16[512,768]{1,0:T(8,128)(2,1)} %param.3), channel_id=1, source_target_pairs={{2,0},{3,1},{4,2},{5,3},{6,4},{7,5},{8,6},{9,7},{10,8},{11,9},{12,... | collective-permute-start | bytes 2359304 | tf_op jit(solution)/shard_map/ppermute | solution.py:16
  8.4 60.5 %collective-permute-start.3 = (bf16[512,768]{1,0:T(8,128)(2,1)}, bf16[512,768]{1,0:T(8,128)(2,1)}, u32[]{:S(2)}, u32[]{:S(2)}) collective-permute-start(bf16[512,768]{1,0:T(8,128)(2,1)} %param.3), channel_id=1, source_target_pairs={{0,2},{1,3},{2,4},{3,5},{4,6},{5,7},{6,8},{7,9},{8,10},{9,11},{10,... | collective-permute-start | bytes 2359304 | tf_op jit(solution)/shard_map/ppermute | solution.py:16
  12.9 86.7 %collective-permute-start.4 = (bf16[512,768]{1,0:T(8,128)(2,1)}, bf16[512,768]{1,0:T(8,128)(2,1)}, u32[]{:S(2)}, u32[]{:S(2)}) collective-permute-start(bf16[512,768]{1,0:T(8,128)(2,1)} %param.3), channel_id=1, source_target_pairs={{3,0},{4,1},{5,2},{6,3},{7,4},{8,5},{9,6},{10,7},{11,8},{12,9},{13... | collective-permute-start | bytes 2359304 | tf_op jit(solution)/shard_map/ppermute | solution.py:16
  15.3 86.4 %collective-permute-start.5 = (bf16[512,768]{1,0:T(8,128)(2,1)}, bf16[512,768]{1,0:T(8,128)(2,1)}, u32[]{:S(2)}, u32[]{:S(2)}) collective-permute-start(bf16[512,768]{1,0:T(8,128)(2,1)} %param.3), channel_id=1, source_target_pairs={{0,3},{1,4},{2,5},{3,6},{4,7},{5,8},{6,9},{7,10},{8,11},{9,12},{10... | collective-permute-start | bytes 2359304 | tf_op jit(solution)/shard_map/ppermute | solution.py:16
  23.2 38.5 %copy-start = (bf16[512,768]{1,0:T(8,128)(2,1)S(1)}, bf16[512,768]{1,0:T(8,128)(2,1)}, u32[]{:S(2)}) copy-start(bf16[512,768]{1,0:T(8,128)(2,1)} %param.3) | copy-start | bytes 2359300
  24.1 79.8 %copy-start.11 = (f32[512,512]{1,0:T(8,128)}, f32[512,512]{1,0:T(8,128)S(1)}, u32[]{:S(2)}) copy-start(f32[512,512]{1,0:T(8,128)S(1)} %copy.6) | copy-start | bytes 3145732
  61.7 42.9 %collective-permute-start.6 = (bf16[512,768]{1,0:T(8,128)(2,1)S(1)}, bf16[512,768]{1,0:T(8,128)(2,1)S(1)}, u32[]{:S(2)}, u32[]{:S(2)}) collective-permute-start(bf16[512,768]{1,0:T(8,128)(2,1)S(1)} %copy-done), channel_id=1, source_target_pairs={{4,0},{5,1},{6,2},{7,3},{8,4},{9,5},{10,6},{11,7},{12,8},{13,9},{1... | collective-permute-start | bytes 2359304 | tf_op jit(solution)/shard_map/ppermute | solution.py:16
  68.9 72.7 %copy-start.1 = (f32[512,512]{1,0:T(8,128)}, f32[512,512]{1,0:T(8,128)S(1)}, u32[]{:S(2)}) copy-start(f32[512,512]{1,0:T(8,128)S(1)} %convolution_multiply_fusion.5) | copy-start | bytes 3145732
  68.9 40.0 %collective-permute-start.7 = (bf16[512,768]{1,0:T(8,128)(2,1)S(1)}, bf16[512,768]{1,0:T(8,128)(2,1)S(1)}, u32[]{:S(2)}, u32[]{:S(2)}) collective-permute-start(bf16[512,768]{1,0:T(8,128)(2,1)S(1)} %copy-done), channel_id=1, source_target_pairs={{0,4},{1,5},{2,6},{3,7},{4,8},{5,9},{6,10},{7,11},{8,12},{9,13},{1... | collective-permute-start | bytes 2359304 | tf_op jit(solution)/shard_map/ppermute | solution.py:16
  75.4 65.7 %copy-start.9 = (f32[512,512]{1,0:T(8,128)}, f32[512,512]{1,0:T(8,128)S(1)}, u32[]{:S(2)}) copy-start(f32[512,512]{1,0:T(8,128)S(1)} %convolution_multiply_fusion.4) | copy-start | bytes 3145732
  75.4 63.9 %collective-permute-start.1 = (bf16[512,768]{1,0:T(8,128)(2,1)S(1)}, bf16[512,768]{1,0:T(8,128)(2,1)S(1)}, u32[]{:S(2)}, u32[]{:S(2)}) collective-permute-start(bf16[512,768]{1,0:T(8,128)(2,1)S(1)} %copy-done), channel_id=1, source_target_pairs={{0,1},{1,2},{2,3},{3,4},{4,5},{5,6},{6,7},{7,8},{8,9},{9,10},{10,1... | collective-permute-start | bytes 2359304 | tf_op jit(solution)/shard_map/ppermute | solution.py:16
  101.8 39.8 %copy-start.3 = (f32[512,512]{1,0:T(8,128)}, f32[512,512]{1,0:T(8,128)S(1)}, u32[]{:S(2)}) copy-start(f32[512,512]{1,0:T(8,128)S(1)} %convolution_multiply_fusion.3) | copy-start | bytes 3145732
  103.9 37.7 %copy-start.5 = (f32[512,512]{1,0:T(8,128)}, f32[512,512]{1,0:T(8,128)S(1)}, u32[]{:S(2)}) copy-start(f32[512,512]{1,0:T(8,128)S(1)} %convolution_multiply_fusion.2) | copy-start | bytes 3145732
  105.2 36.3 %copy-start.7 = (f32[512,512]{1,0:T(8,128)}, f32[512,512]{1,0:T(8,128)S(1)}, u32[]{:S(2)}) copy-start(f32[512,512]{1,0:T(8,128)S(1)} %convolution_multiply_fusion.1) | copy-start | bytes 3145732
  105.3 34.1 %copy-start.12 = (f32[512,512]{1,0:T(8,128)S(1)}, f32[512,512]{1,0:T(8,128)}, u32[]{:S(2)}) copy-start(f32[512,512]{1,0:T(8,128)} %copy-done.11) | copy-start | bytes 3145732
  144.3 24.3 %collective-permute-start.14 = (f32[512]{0:T(512)S(1)}, f32[512]{0:T(512)S(1)}, u32[]{:S(2)}, u32[]{:S(2)}) collective-permute-start(f32[512]{0:T(512)S(1)} %get-tuple-element.20), channel_id=1, source_target_pairs={{4,0},{5,1},{6,2},{7,3},{8,4},{9,5},{10,6},{11,7},{12,8},{13,9},{1... | collective-permute-start | bytes 6152 | tf_op jit(solution)/shard_map/ppermute | solution.py:16
  146.3 28.0 %collective-permute-start.13 = (f32[512]{0:T(512)S(1)}, f32[512]{0:T(512)S(1)}, u32[]{:S(2)}, u32[]{:S(2)}) collective-permute-start(f32[512]{0:T(512)S(1)} %get-tuple-element.20), channel_id=1, source_target_pairs={{0,3},{1,4},{2,5},{3,6},{4,7},{5,8},{6,9},{7,10},{8,11},{9,12},{10... | collective-permute-start | bytes 6152 | tf_op jit(solution)/shard_map/ppermute | solution.py:16
  148.2 32.5 %collective-permute-start.12 = (f32[512]{0:T(512)S(1)}, f32[512]{0:T(512)S(1)}, u32[]{:S(2)}, u32[]{:S(2)}) collective-permute-start(f32[512]{0:T(512)S(1)} %get-tuple-element.20), channel_id=1, source_target_pairs={{3,0},{4,1},{5,2},{6,3},{7,4},{8,5},{9,6},{10,7},{11,8},{12,9},{13... | collective-permute-start | bytes 6152 | tf_op jit(solution)/shard_map/ppermute | solution.py:16
  154.0 43.5 %collective-permute-start.11 = (f32[512]{0:T(512)S(1)}, f32[512]{0:T(512)S(1)}, u32[]{:S(2)}, u32[]{:S(2)}) collective-permute-start(f32[512]{0:T(512)S(1)} %get-tuple-element.20), channel_id=1, source_target_pairs={{0,2},{1,3},{2,4},{3,5},{4,6},{5,7},{6,8},{7,9},{8,10},{9,11},{10,... | collective-permute-start | bytes 6152 | tf_op jit(solution)/shard_map/ppermute | solution.py:16
  155.9 43.7 %collective-permute-start.10 = (f32[512]{0:T(512)S(1)}, f32[512]{0:T(512)S(1)}, u32[]{:S(2)}, u32[]{:S(2)}) collective-permute-start(f32[512]{0:T(512)S(1)} %get-tuple-element.20), channel_id=1, source_target_pairs={{2,0},{3,1},{4,2},{5,3},{6,4},{7,5},{8,6},{9,7},{10,8},{11,9},{12,... | collective-permute-start | bytes 6152 | tf_op jit(solution)/shard_map/ppermute | solution.py:16
  168.6 33.2 %collective-permute-start.9 = (f32[512]{0:T(512)S(1)}, f32[512]{0:T(512)S(1)}, u32[]{:S(2)}, u32[]{:S(2)}) collective-permute-start(f32[512]{0:T(512)S(1)} %get-tuple-element.20), channel_id=1, source_target_pairs={{0,1},{1,2},{2,3},{3,4},{4,5},{5,6},{6,7},{7,8},{8,9},{9,10},{10,1... | collective-permute-start | bytes 6152 | tf_op jit(solution)/shard_map/ppermute | solution.py:16
  174.3 28.5 %collective-permute-start.8 = (f32[512]{0:T(512)S(1)}, f32[512]{0:T(512)S(1)}, u32[]{:S(2)}, u32[]{:S(2)}) collective-permute-start(f32[512]{0:T(512)S(1)} %get-tuple-element.20), channel_id=1, source_target_pairs={{1,0},{2,1},{3,2},{4,3},{5,4},{6,5},{7,6},{8,7},{9,8},{10,9},{11,1... | collective-permute-start | bytes 6152 | tf_op jit(solution)/shard_map/ppermute | solution.py:16
  180.7 24.3 %collective-permute-start.15 = (f32[512]{0:T(512)S(1)}, f32[512]{0:T(512)S(1)}, u32[]{:S(2)}, u32[]{:S(2)}) collective-permute-start(f32[512]{0:T(512)S(1)} %get-tuple-element.20), channel_id=1, source_target_pairs={{0,4},{1,5},{2,6},{3,7},{4,8},{5,9},{6,10},{7,11},{8,12},{9,13},{1... | collective-permute-start | bytes 6152 | tf_op jit(solution)/shard_map/ppermute | solution.py:16
  (17 other events, 140.9 us)
where the time goes:
time: 208 us; the launch traced here: 207 us
  starting transfers between devices  95.7 us (46%)
  waiting for transfers between devices  71 us (34%)
  matrix products  31.4 us (15%)
  other arithmetic  5.07 us (2%)
  local copies, waits for them, and re-layouts  2.83 us (1%)
    ppermute x16, starting transfers between devices, shifted(): lax.ppermute(value, axis, [(source, source + steps) for source in range(l...  95.7 us
    ppermute x16, waiting for transfers between devices, shifted(): lax.ppermute(value, axis, [(source, source + steps) for source in range(l...  71 us
    dot_general x9, matrix products, pair_scores(): lax.dot_general(left, right, (((1,), (1,)), ((), ())), preferred_element_...  14.4 us
    dot_general x4, matrix products, shards(): jnp.dot(weights_back, behind, preferred_element_type=jnp.float32) * scale  7.24 us
    dot_general x4, matrix products, shards(): jnp.dot(weights, ahead, preferred_element_type=jnp.float32) * scale  6.99 us
  transfers between devices with their start and end apart: 16, of which 3 were waited for; matrix products, arithmetic and copies ran while one was open for 15% of the time, Pallas kernels for 0%

commit v1 on v0

v1 whole, which is shorter than its diff:
```python
import functools
import math

import jax
import jax.numpy as jnp
from jax import lax
from jax.experimental import pallas as pl
from jax.experimental.pallas import tpu as pltpu
from jax.sharding import PartitionSpec as P

BLOCK = 256
REACH = 4
MOST = 8
NEG = -1e30
AXES = ("row", "col")


def shifted(value, steps):
    count = lax.axis_size(AXES)
    leading, last = (max(0, -steps), min(count, count - steps))
    return lax.ppermute(value, AXES, [(source, source + steps) for source in range(leading, last)])


def kernel(dev_ref, cluster_ref, shift_ref, *refs):
    slabs = refs[: 2 * REACH + 1]
    loss_ref, grad_ref, window, scores, lse, weights, sems = refs[2 * REACH + 1 :]
    rows, width = slabs[0].shape
    here = rows // BLOCK
    blocks = cluster_ref.shape[0]
    scale = width**-0.5
    log2e = math.log2(math.e)
    copies = [
        pltpu.make_async_copy(slab, window.at[pl.ds(n * rows, rows), :], sems.at[n])
        for n, slab in enumerate(slabs)
    ]
    for copy in copies:
        copy.start()

    first = dev_ref[0] * here - REACH * here

    def cluster_at(w):
        g = first + w
        inside = jnp.logical_and(g >= 0, g < blocks)
        return jnp.where(inside, cluster_ref[jnp.clip(g, 0, blocks - 1)], -1)

    def extent(own):
        mine = cluster_at(own)
        begin, end = jnp.int32(own), jnp.int32(own + 1)
        for step in range(1, MOST):
            begin = jnp.where(cluster_at(own - step) == mine, own - step, begin)
            end = jnp.where(cluster_at(own + step) == mine, own + step + 1, end)
        return begin, end

    begin0, end0 = extent(REACH * here)
    begin1, end1 = extent(REACH * here + 1)
    for copy in copies:
        copy.wait()

    row = lax.broadcasted_iota(jnp.int32, (BLOCK, BLOCK), 0)
    column = lax.broadcasted_iota(jnp.int32, (BLOCK, BLOCK), 1)
    span = MOST * BLOCK

    def at(block):
        return pl.ds(pl.multiple_of(block * BLOCK, BLOCK), BLOCK)

    def upright(values):
        return jnp.sum(jnp.where(row == column, values, 0.0), axis=1, keepdims=True)

    def own_block(r, _):
        begin = jnp.where(r == 0, begin0, begin1)
        length = jnp.where(r == 0, end0, end1) - begin
        own = REACH * here + r - begin

        def statistics(j, _):
            far = window[at(begin + j), :]
            for i in range(MOST):
                tile = lax.dot_general(
                    window[at(begin + i), :],
                    far,
                    (((1,), (1,)), ((), ())),
                    preferred_element_type=jnp.float32,
                )
                scores[j, i * BLOCK : (i + 1) * BLOCK, :] = tile * (scale * log2e)
            scores[j, at(j), :] = jnp.where(row == column, NEG, scores[j, at(j), :])
            top = jnp.full((8, BLOCK), NEG, jnp.float32)
            for i in range(MOST):
                tile = scores[j, i * BLOCK : (i + 1) * BLOCK, :]
                part = jnp.max(tile.reshape(BLOCK // 8, 8, BLOCK), axis=0)
                top = jnp.where(i < length, jnp.maximum(top, part), top)
            top = jnp.max(top, axis=0, keepdims=True)
            total = jnp.zeros((8, BLOCK), jnp.float32)
            for i in range(MOST):
                tile = jnp.exp2(scores[j, i * BLOCK : (i + 1) * BLOCK, :] - top)
                part = jnp.sum(tile.reshape(BLOCK // 8, 8, BLOCK), axis=0)
                total = jnp.where(i < length, total + part, total)
            lse[pl.ds(j, 1), :] = top + jnp.log2(jnp.sum(total, axis=0, keepdims=True))
            return 0

        @pl.when(jnp.logical_or(r == 0, begin0 != begin1))
        def _():
            lax.fori_loop(0, length, statistics, 0)

        mine = lse[pl.ds(own, 1), :]
        mine_up = upright(mine)

        def weigh(j, _):
            tile = scores[j, at(own), :]
            weight = jnp.exp2(tile - mine_up) + jnp.exp2(tile - lse[pl.ds(j, 1), :])
            weights[:, at(j)] = weight.astype(jnp.bfloat16)
            return 0

        def blank(j, _):
            weights[:, at(j)] = jnp.zeros((BLOCK, BLOCK), jnp.bfloat16)
            return 0

        lax.fori_loop(0, length, weigh, 0)
        lax.fori_loop(length, MOST, blank, 0)
        shift = shift_ref[pl.ds(r, 1), :]
        shift_up = upright(shift.astype(jnp.float32)).astype(jnp.int32)
        tile = scores[own, at(own), :]
        behind = row == jnp.bitwise_and(column + shift, BLOCK - 1)
        ahead = column == jnp.bitwise_and(row + shift_up, BLOCK - 1)
        weight = jnp.exp2(tile - mine_up) + jnp.exp2(tile - mine)
        weight = weight - jnp.where(ahead, 1.0, 0.0) - jnp.where(behind, 1.0, 0.0)
        weights[:, at(own)] = weight.astype(jnp.bfloat16)
        positive = jnp.sum(jnp.where(behind, tile, 0.0), axis=0, keepdims=True)
        loss_ref[pl.ds(r, 1), :] = (mine - positive) * (1.0 / log2e)
        total = jnp.dot(
            weights[...],
            window[pl.ds(pl.multiple_of(begin * BLOCK, BLOCK), span), :],
            preferred_element_type=jnp.float32,
        )
        grad_ref[at(r), :] = total * scale
        return 0

    lax.fori_loop(0, here, own_block, 0)


def local_work(device, block_cluster, partner_shift, slabs):
    rows, width = slabs[0].shape
    here = rows // BLOCK
    whole = pl.BlockSpec(memory_space=pltpu.VMEM)
    scalar = pl.BlockSpec(memory_space=pltpu.SMEM)
    loss, grad = pl.pallas_call(
        kernel,
        out_shape=(
            jax.ShapeDtypeStruct((here, BLOCK), jnp.float32),
            jax.ShapeDtypeStruct((rows, width), jnp.float32),
        ),
        in_specs=[scalar, scalar, whole] + [pl.BlockSpec(memory_space=pl.ANY)] * len(slabs),
        out_specs=(whole, whole),
        scratch_shapes=[
            pltpu.VMEM((len(slabs) * rows, width), jnp.bfloat16),
            pltpu.VMEM((MOST, MOST * BLOCK, BLOCK), jnp.float32),
            pltpu.VMEM((MOST, BLOCK), jnp.float32),
            pltpu.VMEM((BLOCK, MOST * BLOCK), jnp.bfloat16),
            pltpu.SemaphoreType.DMA((len(slabs),)),
        ],
        compiler_params=pltpu.CompilerParams(vmem_limit_bytes=48 * 1024 * 1024),
        name="cluster_loss",
    )(device, block_cluster, partner_shift.reshape(here, BLOCK), *slabs)
    return loss.reshape(rows), grad


def shards(embeddings, block_cluster, partner_shift):
    device = lax.axis_index(AXES).astype(jnp.int32).reshape(1)
    slabs = [
        embeddings if offset == 0 else shifted(embeddings, -offset)
        for offset in range(-REACH, REACH + 1)
    ]
    return local_work(device, block_cluster, partner_shift, slabs)


def solution(mesh):
    in_specs = (P(AXES, None), P(), P(AXES))
    out_specs = (P(AXES), P(AXES, None))
    return jax.shard_map(shards, mesh=mesh, in_specs=in_specs, out_specs=out_specs, check_vma=False)
```

time: 208 us -> 156 us (0.75)
  the two profiles are of different devices: /device:TPU:103 before, /device:TPU:233 now
where the time goes in v1:
time: 156 us; the launch traced here: 157 us
  starting transfers between devices  78.8 us (51%)
  waiting for transfers between devices  48.3 us (31%)
  Pallas kernels  25.8 us (17%)
  local copies, waits for them, and re-layouts  3.09 us (2%)
    ppermute x8, starting transfers between devices, shifted(): lax.ppermute(value, AXES, [(source, source + steps) for source in range(l...  78.8 us
    ppermute x8, waiting for transfers between devices, shifted(): lax.ppermute(value, AXES, [(source, source + steps) for source in range(l...  48.3 us
    pallas_call x1, Pallas kernels, local_work(): pl.pallas_call(kernel, out_shape=(jax.ShapeDtypeStruct((here, BLOCK), jnp...  25.8 us
  transfers between devices with their start and end apart: 8, of which 5 were waited for; matrix products, arithmetic and copies ran while one was open for 0% of the time, Pallas kernels for 0%

profile of v1, /device:TPU:233, one launch (start us, length us, event | category | flops | bytes accessed | tf_op | source)
XLA Modules:
  0.0 156.7 jit_solution(16223701540243462731)
XLA Ops:
  0.6 6.2 %collective-permute-start.6 = (bf16[512,768]{1,0:T(8,128)(2,1)}, bf16[512,768]{1,0:T(8,128)(2,1)S(1)}, u32[]{:S(2)}, u32[]{:S(2)}) collective-permute-start(bf16[512,768]{1,0:T(8,128)(2,1)} %refs_4_.1), channel_id=1, source_target_pairs={{3,0},{4,1},{5,2},{6,3},{7,4},{8,5},{9,6},{10,7},{11,8},{12,9},{13... | collective-permute-start | bytes 2359304 | tf_op jit(solution)/shard_map/ppermute | solution.py:21
  6.9 2.9 %collective-permute-start.5 = (bf16[512,768]{1,0:T(8,128)(2,1)}, bf16[512,768]{1,0:T(8,128)(2,1)S(1)}, u32[]{:S(2)}, u32[]{:S(2)}) collective-permute-start(bf16[512,768]{1,0:T(8,128)(2,1)} %refs_4_.1), channel_id=1, source_target_pairs={{2,0},{3,1},{4,2},{5,3},{6,4},{7,5},{8,6},{9,7},{10,8},{11,9},{12,... | collective-permute-start | bytes 2359304 | tf_op jit(solution)/shard_map/ppermute | solution.py:21
  9.7 4.0 %collective-permute-start.4 = (bf16[512,768]{1,0:T(8,128)(2,1)}, bf16[512,768]{1,0:T(8,128)(2,1)S(1)}, u32[]{:S(2)}, u32[]{:S(2)}) collective-permute-start(bf16[512,768]{1,0:T(8,128)(2,1)} %refs_4_.1), channel_id=1, source_target_pairs={{1,0},{2,1},{3,2},{4,3},{5,4},{6,5},{7,6},{8,7},{9,8},{10,9},{11,1... | collective-permute-start | bytes 2359304 | tf_op jit(solution)/shard_map/ppermute | solution.py:21
  13.7 1.9 %collective-permute-start.3 = (bf16[512,768]{1,0:T(8,128)(2,1)}, bf16[512,768]{1,0:T(8,128)(2,1)S(1)}, u32[]{:S(2)}, u32[]{:S(2)}) collective-permute-start(bf16[512,768]{1,0:T(8,128)(2,1)} %refs_4_.1), channel_id=1, source_target_pairs={{0,1},{1,2},{2,3},{3,4},{4,5},{5,6},{6,7},{7,8},{8,9},{9,10},{10,1... | collective-permute-start | bytes 2359304 | tf_op jit(solution)/shard_map/ppermute | solution.py:21
  15.6 6.9 %collective-permute-start.2 = (bf16[512,768]{1,0:T(8,128)(2,1)}, bf16[512,768]{1,0:T(8,128)(2,1)S(1)}, u32[]{:S(2)}, u32[]{:S(2)}) collective-permute-start(bf16[512,768]{1,0:T(8,128)(2,1)} %refs_4_.1), channel_id=1, source_target_pairs={{0,2},{1,3},{2,4},{3,5},{4,6},{5,7},{6,8},{7,9},{8,10},{9,11},{10,... | collective-permute-start | bytes 2359304 | tf_op jit(solution)/shard_map/ppermute | solution.py:21
  22.6 3.4 %collective-permute-done.6.refs_7_ = bf16[512,768]{1,0:T(8,128)(2,1)S(1)} collective-permute-done((bf16[512,768]{1,0:T(8,128)(2,1)}, bf16[512,768]{1,0:T(8,128)(2,1)S(1)}, u32[]{:S(2)}, u32[]{:S(2)}) %collective-permute-start.6) | collective-permute-done | bytes 786464 | tf_op jit(solution)/shard_map/ppermute | solution.py:21
  26.0 0.0 copy-start.2
  26.0 51.2 %collective-permute-start.1 = (bf16[512,768]{1,0:T(8,128)(2,1)}, bf16[512,768]{1,0:T(8,128)(2,1)}, u32[]{:S(2)}, u32[]{:S(2)}) collective-permute-start(bf16[512,768]{1,0:T(8,128)(2,1)} %refs_4_.1), channel_id=1, source_target_pairs={{0,3},{1,4},{2,5},{3,6},{4,7},{5,8},{6,9},{7,10},{8,11},{9,12},{10... | collective-permute-start | bytes 2359304 | tf_op jit(solution)/shard_map/ppermute | solution.py:21
  77.2 0.0 collective-permute-done.5.refs_6_
  77.2 1.9 %collective-permute-start = (bf16[512,768]{1,0:T(8,128)(2,1)}, bf16[512,768]{1,0:T(8,128)(2,1)}, u32[]{:S(2)}, u32[]{:S(2)}) collective-permute-start(bf16[512,768]{1,0:T(8,128)(2,1)} %refs_4_.1), channel_id=1, source_target_pairs={{0,4},{1,5},{2,6},{3,7},{4,8},{5,9},{6,10},{7,11},{8,12},{9,13},{1... | collective-permute-start | bytes 2359304 | tf_op jit(solution)/shard_map/ppermute | solution.py:21
  79.2 1.4 collective-permute-done.4.refs_5_
  80.5 0.0 copy-done.2
  80.5 3.8 %collective-permute-start.7 = (bf16[512,768]{1,0:T(8,128)(2,1)}, bf16[512,768]{1,0:T(8,128)(2,1)}, u32[]{:S(2)}, u32[]{:S(2)}) collective-permute-start(bf16[512,768]{1,0:T(8,128)(2,1)} %refs_4_.1), channel_id=1, source_target_pairs={{4,0},{5,1},{6,2},{7,3},{8,4},{9,5},{10,6},{11,7},{12,8},{13,9},{1... | collective-permute-start | bytes 2359304 | tf_op jit(solution)/shard_map/ppermute | solution.py:21
  84.4 0.7 reshape.14.shift_ref
  85.1 0.0 collective-permute-done.3.refs_3_
  85.1 0.0 collective-permute-done.2.refs_2_
  85.1 15.8 %collective-permute-done.1.refs_1_ = bf16[512,768]{1,0:T(8,128)(2,1)} collective-permute-done((bf16[512,768]{1,0:T(8,128)(2,1)}, bf16[512,768]{1,0:T(8,128)(2,1)}, u32[]{:S(2)}, u32[]{:S(2)}) %collective-permute-start.1) | collective-permute-done | bytes 786464 | tf_op jit(solution)/shard_map/ppermute | solution.py:21
  100.9 16.9 %collective-permute-done.refs_0_ = bf16[512,768]{1,0:T(8,128)(2,1)} collective-permute-done((bf16[512,768]{1,0:T(8,128)(2,1)}, bf16[512,768]{1,0:T(8,128)(2,1)}, u32[]{:S(2)}, u32[]{:S(2)}) %collective-permute-start) | collective-permute-done | bytes 786464 | tf_op jit(solution)/shard_map/ppermute | solution.py:21
  117.8 10.8 %collective-permute-done.7.refs_8_ = bf16[512,768]{1,0:T(8,128)(2,1)} collective-permute-done((bf16[512,768]{1,0:T(8,128)(2,1)}, bf16[512,768]{1,0:T(8,128)(2,1)}, u32[]{:S(2)}, u32[]{:S(2)}) %collective-permute-start.7) | collective-permute-done | bytes 786464 | tf_op jit(solution)/shard_map/ppermute | solution.py:21
  128.5 0.0 copy-start
  128.5 1.1 copy-done
  129.7 0.7 copy-done.1
  130.4 25.8 %cluster_loss.1 = (f32[2,256]{1,0:T(2,128)S(1)}, f32[512,768]{1,0:T(8,128)}) custom-call(s32[1]{0:T(128)} %bitcast.dev_ref, s32[512]{0:T(512)S(1)} %copy-done.1, s32[2,256]{1,0:T(2,128)S(1)} %reshape.14.shift_ref, bf16[512,768]{1,0:T(8,128)(2,1)} %collective-permute-done.refs_0_, bf16[512,768]{1,0:T(8,128)(2,1)} %collective-permute-done.1.refs_1_, ...), custom_call_target="tpu_custom_call" | custom-call | tf_op jit(solution)/shard_map/cluster_loss/pallas_call | solution.py:144
  156.1 0.6 copy.5
  (1 shorter events, 0.0 us)
Async XLA Ops:
  0.6 25.4 %collective-permute-start.6 = (bf16[512,768]{1,0:T(8,128)(2,1)}, bf16[512,768]{1,0:T(8,128)(2,1)S(1)}, u32[]{:S(2)}, u32[]{:S(2)}) collective-permute-start(bf16[512,768]{1,0:T(8,128)(2,1)} %refs_4_.1), channel_id=1, source_target_pairs={{3,0},{4,1},{5,2},{6,3},{7,4},{8,5},{9,6},{10,7},{11,8},{12,9},{13... | collective-permute-start | bytes 2359304 | tf_op jit(solution)/shard_map/ppermute | solution.py:21
  6.9 70.4 %collective-permute-start.5 = (bf16[512,768]{1,0:T(8,128)(2,1)}, bf16[512,768]{1,0:T(8,128)(2,1)S(1)}, u32[]{:S(2)}, u32[]{:S(2)}) collective-permute-start(bf16[512,768]{1,0:T(8,128)(2,1)} %refs_4_.1), channel_id=1, source_target_pairs={{2,0},{3,1},{4,2},{5,3},{6,4},{7,5},{8,6},{9,7},{10,8},{11,9},{12,... | collective-permute-start | bytes 2359304 | tf_op jit(solution)/shard_map/ppermute | solution.py:21
  9.7 70.8 %collective-permute-start.4 = (bf16[512,768]{1,0:T(8,128)(2,1)}, bf16[512,768]{1,0:T(8,128)(2,1)S(1)}, u32[]{:S(2)}, u32[]{:S(2)}) collective-permute-start(bf16[512,768]{1,0:T(8,128)(2,1)} %refs_4_.1), channel_id=1, source_target_pairs={{1,0},{2,1},{3,2},{4,3},{5,4},{6,5},{7,6},{8,7},{9,8},{10,9},{11,1... | collective-permute-start | bytes 2359304 | tf_op jit(solution)/shard_map/ppermute | solution.py:21
  13.7 71.3 %collective-permute-start.3 = (bf16[512,768]{1,0:T(8,128)(2,1)}, bf16[512,768]{1,0:T(8,128)(2,1)S(1)}, u32[]{:S(2)}, u32[]{:S(2)}) collective-permute-start(bf16[512,768]{1,0:T(8,128)(2,1)} %refs_4_.1), channel_id=1, source_target_pairs={{0,1},{1,2},{2,3},{3,4},{4,5},{5,6},{6,7},{7,8},{8,9},{9,10},{10,1... | collective-permute-start | bytes 2359304 | tf_op jit(solution)/shard_map/ppermute | solution.py:21
  15.6 69.4 %collective-permute-start.2 = (bf16[512,768]{1,0:T(8,128)(2,1)}, bf16[512,768]{1,0:T(8,128)(2,1)S(1)}, u32[]{:S(2)}, u32[]{:S(2)}) collective-permute-start(bf16[512,768]{1,0:T(8,128)(2,1)} %refs_4_.1), channel_id=1, source_target_pairs={{0,2},{1,3},{2,4},{3,5},{4,6},{5,7},{6,8},{7,9},{8,10},{9,11},{10,... | collective-permute-start | bytes 2359304 | tf_op jit(solution)/shard_map/ppermute | solution.py:21
  26.0 54.5 %copy-start.2 = (bf16[512,768]{1,0:T(8,128)(2,1)}, bf16[512,768]{1,0:T(8,128)(2,1)S(1)}, u32[]{:S(2)}) copy-start(bf16[512,768]{1,0:T(8,128)(2,1)S(1)} %collective-permute-done.6.refs_7_) | copy-start | bytes 2359300
  26.0 74.9 %collective-permute-start.1 = (bf16[512,768]{1,0:T(8,128)(2,1)}, bf16[512,768]{1,0:T(8,128)(2,1)}, u32[]{:S(2)}, u32[]{:S(2)}) collective-permute-start(bf16[512,768]{1,0:T(8,128)(2,1)} %refs_4_.1), channel_id=1, source_target_pairs={{0,3},{1,4},{2,5},{3,6},{4,7},{5,8},{6,9},{7,10},{8,11},{9,12},{10... | collective-permute-start | bytes 2359304 | tf_op jit(solution)/shard_map/ppermute | solution.py:21
  77.2 40.5 %collective-permute-start = (bf16[512,768]{1,0:T(8,128)(2,1)}, bf16[512,768]{1,0:T(8,128)(2,1)}, u32[]{:S(2)}, u32[]{:S(2)}) collective-permute-start(bf16[512,768]{1,0:T(8,128)(2,1)} %refs_4_.1), channel_id=1, source_target_pairs={{0,4},{1,5},{2,6},{3,7},{4,8},{5,9},{6,10},{7,11},{8,12},{9,13},{1... | collective-permute-start | bytes 2359304 | tf_op jit(solution)/shard_map/ppermute | solution.py:21
  80.5 48.0 %collective-permute-start.7 = (bf16[512,768]{1,0:T(8,128)(2,1)}, bf16[512,768]{1,0:T(8,128)(2,1)}, u32[]{:S(2)}, u32[]{:S(2)}) collective-permute-start(bf16[512,768]{1,0:T(8,128)(2,1)} %refs_4_.1), channel_id=1, source_target_pairs={{4,0},{5,1},{6,2},{7,3},{8,4},{9,5},{10,6},{11,7},{12,8},{13,9},{1... | collective-permute-start | bytes 2359304 | tf_op jit(solution)/shard_map/ppermute | solution.py:21
  128.5 1.1 copy-start
  129.7 0.7 copy-start.1

commit v2 on v1

--- a/solution.py
+++ b/solution.py
@@ -10,15 +10,42 @@
 
 BLOCK = 256
 REACH = 4
+LINE = 4
 MOST = 8
 NEG = -1e30
 AXES = ("row", "col")
 
 
-def shifted(value, steps):
+def moved(value, target):
     count = lax.axis_size(AXES)
-    leading, last = (max(0, -steps), min(count, count - steps))
-    return lax.ppermute(value, AXES, [(source, source + steps) for source in range(leading, last)])
+    pairs = [(source, target(source // LINE, source % LINE)) for source in range(count)]
+    pairs = [(source, line * LINE + place) for source, (line, place) in pairs]
+    return lax.ppermute(value, AXES, [(s, t) for s, t in pairs if 0 <= t < count])
+
+
+def around(value, steps):
+    return moved(value, lambda line, place: (line, (place + steps) % LINE))
+
+
+def exchange(own, place):
+    late = moved(own, lambda line, place: (line + 1 if place == LINE - 1 else line - 1, place))
+    early = moved(own, lambda line, place: (line - 1 if place == LINE - 1 else line + 1, place))
+    across = around(own, 2)
+    up = around(own, 1)
+    down = around(own, -1)
+    crossed = moved(across, lambda line, place: (line - 1 if place >= 2 else line + 1, place))
+    late_up = around(late, 1)
+    inner = jnp.logical_or(place == 1, place == 2)
+    early_down = around(jnp.where(inner, early, late), -1)
+    return [own, late, early, across, up, down, crossed, late_up, early_down]
+
+
+def slots(place):
+    late = jnp.where(place < 3, 8, 0)
+    across = jnp.where(place >= 2, 2, 6)
+    up = jnp.where(place >= 1, 3, 7)
+    down = jnp.where(place <= 2, 5, 1)
+    return [4, late, 8 - late, across, up, down, 8 - across, 10 - up, 6 - down]
 
 
 def kernel(dev_ref, cluster_ref, shift_ref, *refs):
@@ -29,9 +56,12 @@
     blocks = cluster_ref.shape[0]
     scale = width**-0.5
     log2e = math.log2(math.e)
+    places = slots(lax.rem(dev_ref[0], LINE))
     copies = [
-        pltpu.make_async_copy(slab, window.at[pl.ds(n * rows, rows), :], sems.at[n])
-        for n, slab in enumerate(slabs)
+        pltpu.make_async_copy(
+            slab, window.at[pl.ds(pl.multiple_of(place * rows, rows), rows), :], sems.at[n]
+        )
+        for n, (slab, place) in enumerate(zip(slabs, places))
     ]
     for copy in copies:
         copy.start()
@@ -164,10 +194,7 @@
 
 def shards(embeddings, block_cluster, partner_shift):
     device = lax.axis_index(AXES).astype(jnp.int32).reshape(1)
-    slabs = [
-        embeddings if offset == 0 else shifted(embeddings, -offset)
-        for offset in range(-REACH, REACH + 1)
-    ]
+    slabs = exchange(embeddings, lax.rem(lax.axis_index("col"), LINE))
     return local_work(device, block_cluster, partner_shift, slabs)
 
 

time: 156 us -> 100 us (0.64)
  the two profiles are of different devices: /device:TPU:233 before, /device:TPU:212 now
where the time goes in v2:
time: 100 us; the launch traced here: 102 us
  waiting for transfers between devices  54.4 us (54%)
  Pallas kernels  30.6 us (31%)
  starting transfers between devices  14.8 us (15%)
    ppermute x8, waiting for transfers between devices, moved(): lax.ppermute(value, AXES, [(s, t) for s, t in pairs if 0 <= t < count])  54.4 us
    pallas_call x1, Pallas kernels, local_work(): pl.pallas_call(kernel, out_shape=(jax.ShapeDtypeStruct((here, BLOCK), jnp...  30.6 us
    ppermute x8, starting transfers between devices, moved(): lax.ppermute(value, AXES, [(s, t) for s, t in pairs if 0 <= t < count])  14.8 us
  transfers between devices with their start and end apart: 8, of which 5 were waited for; matrix products, arithmetic and copies ran while one was open for 1% of the time, Pallas kernels for 0%

profile of v2, /device:TPU:212, one launch (start us, length us, event | category | flops | bytes accessed | tf_op | source)
XLA Modules:
  0.0 102.0 jit_solution(15780513965789063330)
XLA Ops:
  0.6 0.0 copy-start
  0.6 0.0 copy-start.2
  0.6 0.0 copy-start.1
  0.7 0.4 collective-permute-start.2
  1.1 1.9 %collective-permute-start.1 = (bf16[512,768]{1,0:T(8,128)(2,1)}, bf16[512,768]{1,0:T(8,128)(2,1)S(1)}, u32[]{:S(2)}, u32[]{:S(2)}) collective-permute-start(bf16[512,768]{1,0:T(8,128)(2,1)} %refs_0_.1), channel_id=1, source_target_pairs={{0,4},{1,5},{2,6},{4,8},{5,9},{6,10},{7,3},{8,12},{9,13},{10,14},{... | collective-permute-start | bytes 2359304 | tf_op jit(solution)/shard_map/ppermute | solution.py:23
  3.0 5.4 %collective-permute-start = (bf16[512,768]{1,0:T(8,128)(2,1)}, bf16[512,768]{1,0:T(8,128)(2,1)S(1)}, u32[]{:S(2)}, u32[]{:S(2)}) collective-permute-start(bf16[512,768]{1,0:T(8,128)(2,1)} %refs_0_.1), channel_id=1, source_target_pairs={{3,7},{4,0},{5,1},{6,2},{7,11},{8,4},{9,5},{10,6},{11,15},{12,8},{... | collective-permute-start | bytes 2359304 | tf_op jit(solution)/shard_map/ppermute | solution.py:23
  8.4 2.0 %collective-permute-start.3 = (bf16[512,768]{1,0:T(8,128)(2,1)}, bf16[512,768]{1,0:T(8,128)(2,1)}, u32[]{:S(2)}, u32[]{:S(2)}) collective-permute-start(bf16[512,768]{1,0:T(8,128)(2,1)} %refs_0_.1), channel_id=1, source_target_pairs={{0,1},{1,2},{2,3},{3,0},{4,5},{5,6},{6,7},{7,4},{8,9},{9,10},{10,1... | collective-permute-start | bytes 2359304 | tf_op jit(solution)/shard_map/ppermute | solution.py:23
  10.4 0.6 collective-permute-start.4
  11.0 11.9 %collective-permute-done.2.refs_3_ = bf16[512,768]{1,0:T(8,128)(2,1)S(1)} collective-permute-done((bf16[512,768]{1,0:T(8,128)(2,1)}, bf16[512,768]{1,0:T(8,128)(2,1)S(1)}, u32[]{:S(2)}, u32[]{:S(2)}) %collective-permute-start.2) | collective-permute-done | bytes 786464 | tf_op jit(solution)/shard_map/ppermute | solution.py:23
  22.9 2.4 %collective-permute-start.5 = (bf16[512,768]{1,0:T(8,128)(2,1)S(1)}, bf16[512,768]{1,0:T(8,128)(2,1)}, u32[]{:S(2)}, u32[]{:S(2)}) collective-permute-start(bf16[512,768]{1,0:T(8,128)(2,1)S(1)} %collective-permute-done.2.refs_3_), channel_id=1, source_target_pairs={{0,4},{1,5},{4,8},{5,9},{6,2},{7,3},{8,12},{9,13},{10,6},{11,7},{1... | collective-permute-start | bytes 2359304 | tf_op jit(solution)/shard_map/ppermute | solution.py:23
  25.3 16.6 %collective-permute-done.1.refs_2_ = bf16[512,768]{1,0:T(8,128)(2,1)S(1)} collective-permute-done((bf16[512,768]{1,0:T(8,128)(2,1)}, bf16[512,768]{1,0:T(8,128)(2,1)S(1)}, u32[]{:S(2)}, u32[]{:S(2)}) %collective-permute-start.1) | collective-permute-done | bytes 786464 | tf_op jit(solution)/shard_map/ppermute | solution.py:23
  42.0 7.1 %collective-permute-done.refs_1_ = bf16[512,768]{1,0:T(8,128)(2,1)S(1)} collective-permute-done((bf16[512,768]{1,0:T(8,128)(2,1)}, bf16[512,768]{1,0:T(8,128)(2,1)S(1)}, u32[]{:S(2)}, u32[]{:S(2)}) %collective-permute-start) | collective-permute-done | bytes 786464 | tf_op jit(solution)/shard_map/ppermute | solution.py:23
  49.1 1.0 broadcast_select_fusion
  50.1 0.8 collective-permute-start.7
  50.9 1.2 %collective-permute-start.6 = (bf16[512,768]{1,0:T(8,128)(2,1)S(1)}, bf16[512,768]{1,0:T(8,128)(2,1)}, u32[]{:S(2)}, u32[]{:S(2)}) collective-permute-start(bf16[512,768]{1,0:T(8,128)(2,1)S(1)} %collective-permute-done.refs_1_), channel_id=1, source_target_pairs={{0,1},{1,2},{2,3},{3,0},{4,5},{5,6},{6,7},{7,4},{8,9},{9,10},{10,1... | collective-permute-start | bytes 2359304 | tf_op jit(solution)/shard_map/ppermute | solution.py:23
  52.1 0.0 copy-done.2
  52.1 0.0 collective-permute-done.3.refs_4_
  52.1 0.0 collective-permute-done.4.refs_5_
  52.1 5.5 %collective-permute-done.5.refs_6_ = bf16[512,768]{1,0:T(8,128)(2,1)} collective-permute-done((bf16[512,768]{1,0:T(8,128)(2,1)S(1)}, bf16[512,768]{1,0:T(8,128)(2,1)}, u32[]{:S(2)}, u32[]{:S(2)}) %collective-permute-start.5) | collective-permute-done | bytes 786464 | tf_op jit(solution)/shard_map/ppermute | solution.py:23
  57.6 13.2 %collective-permute-done.7.refs_8_ = bf16[512,768]{1,0:T(8,128)(2,1)} collective-permute-done((bf16[512,768]{1,0:T(8,128)(2,1)}, bf16[512,768]{1,0:T(8,128)(2,1)}, u32[]{:S(2)}, u32[]{:S(2)}) %collective-permute-start.7) | collective-permute-done | bytes 786464 | tf_op jit(solution)/shard_map/ppermute | solution.py:23
  70.8 0.0 collective-permute-done.6.refs_7_
  70.8 0.0 copy-done.1
  70.8 30.6 %cluster_loss.1 = (f32[2,256]{1,0:T(2,128)S(1)}, f32[512,768]{1,0:T(8,128)}) custom-call(s32[1]{0:T(128)} %bitcast.dev_ref, s32[512]{0:T(512)S(1)} %copy-done.1, s32[2,256]{1,0:T(2,128)S(1)} %reshape.14.shift_ref, bf16[512,768]{1,0:T(8,128)(2,1)S(1)} %copy-done, bf16[512,768]{1,0:T(8,128)(2,1)S(1)} %collective-permute-done.refs_1_, ...), custom_call_target="tpu_custom_call" | custom-call | tf_op jit(solution)/shard_map/cluster_loss/pallas_call | solution.py:174
  101.4 0.6 copy.5
  (2 shorter events, 0.0 us)
Async XLA Ops:
  0.6 70.2 %copy-start = (bf16[512,768]{1,0:T(8,128)(2,1)S(1)}, bf16[512,768]{1,0:T(8,128)(2,1)}, u32[]{:S(2)}) copy-start(bf16[512,768]{1,0:T(8,128)(2,1)} %refs_0_.1) | copy-start | bytes 2359300
  0.6 51.4 %copy-start.2 = (s32[512]{0:T(512)S(1)}, s32[512]{0:T(512)}, u32[]{:S(2)}) copy-start(s32[512]{0:T(512)} %param.5) | copy-start | bytes 6148
  0.6 70.1 %copy-start.1 = (s32[512]{0:T(512)S(1)}, s32[512]{0:T(512)}, u32[]{:S(2)}) copy-start(s32[512]{0:T(512)} %cluster_ref.1) | copy-start | bytes 6148
  0.7 22.3 %collective-permute-start.2 = (bf16[512,768]{1,0:T(8,128)(2,1)}, bf16[512,768]{1,0:T(8,128)(2,1)S(1)}, u32[]{:S(2)}, u32[]{:S(2)}) collective-permute-start(bf16[512,768]{1,0:T(8,128)(2,1)} %refs_0_.1), channel_id=1, source_target_pairs={{0,2},{1,3},{2,0},{3,1},{4,6},{5,7},{6,4},{7,5},{8,10},{9,11},{10,... | collective-permute-start | bytes 2359304 | tf_op jit(solution)/shard_map/ppermute | solution.py:23
  1.1 40.9 %collective-permute-start.1 = (bf16[512,768]{1,0:T(8,128)(2,1)}, bf16[512,768]{1,0:T(8,128)(2,1)S(1)}, u32[]{:S(2)}, u32[]{:S(2)}) collective-permute-start(bf16[512,768]{1,0:T(8,128)(2,1)} %refs_0_.1), channel_id=1, source_target_pairs={{0,4},{1,5},{2,6},{4,8},{5,9},{6,10},{7,3},{8,12},{9,13},{10,14},{... | collective-permute-start | bytes 2359304 | tf_op jit(solution)/shard_map/ppermute | solution.py:23
  3.0 46.1 %collective-permute-start = (bf16[512,768]{1,0:T(8,128)(2,1)}, bf16[512,768]{1,0:T(8,128)(2,1)S(1)}, u32[]{:S(2)}, u32[]{:S(2)}) collective-permute-start(bf16[512,768]{1,0:T(8,128)(2,1)} %refs_0_.1), channel_id=1, source_target_pairs={{3,7},{4,0},{5,1},{6,2},{7,11},{8,4},{9,5},{10,6},{11,15},{12,8},{... | collective-permute-start | bytes 2359304 | tf_op jit(solution)/shard_map/ppermute | solution.py:23
  8.4 43.7 %collective-permute-start.3 = (bf16[512,768]{1,0:T(8,128)(2,1)}, bf16[512,768]{1,0:T(8,128)(2,1)}, u32[]{:S(2)}, u32[]{:S(2)}) collective-permute-start(bf16[512,768]{1,0:T(8,128)(2,1)} %refs_0_.1), channel_id=1, source_target_pairs={{0,1},{1,2},{2,3},{3,0},{4,5},{5,6},{6,7},{7,4},{8,9},{9,10},{10,1... | collective-permute-start | bytes 2359304 | tf_op jit(solution)/shard_map/ppermute | solution.py:23
  10.4 41.7 %collective-permute-start.4 = (bf16[512,768]{1,0:T(8,128)(2,1)}, bf16[512,768]{1,0:T(8,128)(2,1)}, u32[]{:S(2)}, u32[]{:S(2)}) collective-permute-start(bf16[512,768]{1,0:T(8,128)(2,1)} %refs_0_.1), channel_id=1, source_target_pairs={{0,3},{1,0},{2,1},{3,2},{4,7},{5,4},{6,5},{7,6},{8,11},{9,8},{10,9... | collective-permute-start | bytes 2359304 | tf_op jit(solution)/shard_map/ppermute | solution.py:23
  22.9 34.7 %collective-permute-start.5 = (bf16[512,768]{1,0:T(8,128)(2,1)S(1)}, bf16[512,768]{1,0:T(8,128)(2,1)}, u32[]{:S(2)}, u32[]{:S(2)}) collective-permute-start(bf16[512,768]{1,0:T(8,128)(2,1)S(1)} %collective-permute-done.2.refs_3_), channel_id=1, source_target_pairs={{0,4},{1,5},{4,8},{5,9},{6,2},{7,3},{8,12},{9,13},{10,6},{11,7},{1... | collective-permute-start | bytes 2359304 | tf_op jit(solution)/shard_map/ppermute | solution.py:23
  50.1 20.7 %collective-permute-start.7 = (bf16[512,768]{1,0:T(8,128)(2,1)}, bf16[512,768]{1,0:T(8,128)(2,1)}, u32[]{:S(2)}, u32[]{:S(2)}) collective-permute-start(bf16[512,768]{1,0:T(8,128)(2,1)} %broadcast_select_fusion), channel_id=1, source_target_pairs={{0,3},{1,0},{2,1},{3,2},{4,7},{5,4},{6,5},{7,6},{8,11},{9,8},{10,9... | collective-permute-start | bytes 2359304 | tf_op jit(solution)/shard_map/ppermute | solution.py:23
  50.9 19.9 %collective-permute-start.6 = (bf16[512,768]{1,0:T(8,128)(2,1)S(1)}, bf16[512,768]{1,0:T(8,128)(2,1)}, u32[]{:S(2)}, u32[]{:S(2)}) collective-permute-start(bf16[512,768]{1,0:T(8,128)(2,1)S(1)} %collective-permute-done.refs_1_), channel_id=1, source_target_pairs={{0,1},{1,2},{2,3},{3,0},{4,5},{5,6},{6,7},{7,4},{8,9},{9,10},{10,1... | collective-permute-start | bytes 2359304 | tf_op jit(solution)/shard_map/ppermute | solution.py:23

commit v3 on v1

v3 whole, which is shorter than its diff:
```python
import functools
import math

import jax
import jax.numpy as jnp
from jax import lax
from jax.experimental import pallas as pl
from jax.experimental.pallas import tpu as pltpu
from jax.sharding import PartitionSpec as P

BLOCK = 256
REACH = 4
LINE = 4
MOST = 8
NEG = -1e30
AXES = ("row", "col")


def moved(value, target):
    count = lax.axis_size(AXES)
    pairs = [(source, target(source // LINE, source % LINE)) for source in range(count)]
    pairs = [(source, to[0] * LINE + to[1]) for source, to in pairs if to is not None]
    return lax.ppermute(value, AXES, [(source, to % count) for source, to in pairs])


def parity(line):
    return line // 2 % 2


def exchange(own, *ready):
    late = moved(own, lambda line, at: (line + 1 if at == LINE - 1 else line - 1, at))
    near = moved(own, lambda line, at: (line, (at + (1 if (at + parity(line)) % 2 else -1)) % LINE))
    other = moved(own, lambda line, at: (line, (at - (1 if (at + parity(line)) % 2 else -1)) % LINE))
    across = moved(near, lambda line, at: (line, (at - (1 if (at + parity(line)) % 2 else -1)) % LINE))
    late_sent, *ready = lax.optimization_barrier((late, *ready))
    early = moved(late_sent, lambda line, at: (line - 2 if at == LINE - 1 else line + 2, at))
    late_up = moved(late, lambda line, at: (line, (at + 1) % LINE))
    late_down = moved(late, lambda line, at: (line, at - 1) if at == 3 else (line, 3) if at == 0 else None)
    early_down = moved(early, lambda line, at: (line, at - 1) if at in (1, 2) else None)
    crossed = moved(across, lambda line, at: (line - 1 if at >= 2 else line + 1, at))
    slabs = [own, late, early, across, near, other, crossed, late_up, late_down, early_down]
    return slabs, ready


def slots(device):
    at = lax.rem(device, LINE)
    late = jnp.where(at < 3, 8, 0)
    across = jnp.where(at >= 2, 2, 6)
    from_before = jnp.where(at >= 1, 3, 7)
    from_after = jnp.where(at <= 2, 5, 1)
    before = lax.rem(at + lax.rem(lax.div(device, 2 * LINE), 2), 2) == 0
    near = jnp.where(before, from_before, from_after)
    other = jnp.where(before, from_after, from_before)
    down = 6 - from_after
    where = [4, late, 8 - late, across, near, other, 8 - across, 10 - from_before, down, down]
    return where, [None] * 8 + [at >= 2, at < 2]


def stage(here, new_slots, prior_slots, first, last, refs):
    info_ref, refs = refs[0], refs[1:]
    slabs, refs = refs[: len(new_slots)], refs[len(new_slots) :]
    if last:
        shift_ref, refs = refs[0], refs[1:]
    if not first:
        refs = refs[4:]
    if last:
        loss_ref, grad_ref, refs = refs[0], refs[1], refs[2:]
    window, kept, tops, totals, scores, sems = refs[:6]
    if last:
        lse, weights = refs[6:]
    rows, width = slabs[0].shape
    scale = width**-0.5
    log2e = math.log2(math.e)
    all_slots, taken = slots(info_ref[0])
    copies = [
        pltpu.make_async_copy(
            slab,
            window.at[pl.ds(pl.multiple_of(all_slots[n] * rows, rows), rows), :],
            sems.at[k],
        )
        for k, (slab, n) in enumerate(zip(slabs, new_slots))
    ]
    copies = [(taken[n], copy) for n, copy in zip(new_slots, copies)]

    def each(act):
        for wanted, copy in copies:
            if wanted is None:
                act(copy)
            else:
                pl.when(wanted)(lambda copy=copy: act(copy))

    each(lambda copy: copy.start())

    def mask_of(ids):
        mask = jnp.int32(0)
        for n in ids:
            mask = jnp.bitwise_or(mask, lax.shift_left(jnp.int32(1), jnp.int32(all_slots[n])))
        return mask

    new_mask, prior_mask = mask_of(new_slots), mask_of(prior_slots)

    def held(mask, w):
        return jnp.bitwise_and(lax.shift_right_logical(mask, lax.div(w, here)), 1) == 1

    begin0, end0, begin1, end1 = [info_ref[n] for n in range(1, 5)]
    each(lambda copy: copy.wait())

    row = lax.broadcasted_iota(jnp.int32, (BLOCK, BLOCK), 0)
    column = lax.broadcasted_iota(jnp.int32, (BLOCK, BLOCK), 1)
    span = MOST * BLOCK
    same = begin0 == begin1

    def at(block):
        return pl.ds(pl.multiple_of(block * BLOCK, BLOCK), BLOCK)

    def folded(op, tile):
        return op(tile.reshape(BLOCK // 8, 8, BLOCK), axis=0)

    def upright(values):
        return jnp.sum(jnp.where(row == column, values, 0.0), axis=1, keepdims=True)

    def product(left, right):
        return lax.dot_general(
            window[at(left), :],
            window[at(right), :],
            (((1,), (1,)), ((), ())),
            preferred_element_type=jnp.float32,
        ) * (scale * log2e)

    def own_block(r, _):
        begin = jnp.where(r == 0, begin0, begin1)
        length = jnp.where(r == 0, end0, end1) - begin
        own = REACH * here + r - begin

        def live(i, mask):
            return jnp.logical_and(i < length, held(mask, begin + i))

        def column_strip(j, _):
            @pl.when(held(new_mask, begin + j))
            def _():
                for i in range(MOST):
                    scores[i * BLOCK : (i + 1) * BLOCK, :] = product(begin + i, begin + j)
                scores[at(j), :] = jnp.where(row == column, NEG, scores[at(j), :])
                top = jnp.full((8, BLOCK), NEG, jnp.float32)
                for i in range(MOST):
                    part = folded(jnp.max, scores[i * BLOCK : (i + 1) * BLOCK, :])
                    there = live(i, new_mask + prior_mask)
                    top = jnp.where(there, jnp.maximum(top, part), top)
                top = jnp.max(top, axis=0, keepdims=True)
                total = jnp.zeros((8, BLOCK), jnp.float32)
                for i in range(MOST):
                    part = folded(jnp.sum, jnp.exp2(scores[i * BLOCK : (i + 1) * BLOCK, :] - top))
                    there = live(i, new_mask + prior_mask)
                    total = jnp.where(there, total + part, total)
                tops[pl.ds(r * MOST + j, 1), :] = top
                totals[pl.ds(r * MOST + j, 1), :] = jnp.sum(total, axis=0, keepdims=True)
                kept[r, j] = scores[at(own), :]

                @pl.when(same)
                def _():
                    kept[1, j] = scores[at(own + 1), :]

                if first:
                    return
                for i in range(MOST):

                    @pl.when(live(i, prior_mask))
                    def _():
                        tile = scores[i * BLOCK : (i + 1) * BLOCK, :].T
                        line = pl.ds(r * MOST + i, 1)
                        old = tops[line, :]
                        part = jnp.max(folded(jnp.max, tile), axis=0, keepdims=True)
                        top = jnp.maximum(old, part)
                        part = jnp.sum(folded(jnp.sum, jnp.exp2(tile - top)), axis=0, keepdims=True)
                        totals[line, :] = totals[line, :] * jnp.exp2(old - top) + part
                        tops[line, :] = top

            return 0

        @pl.when(jnp.logical_or(r == 0, jnp.logical_not(same)))
        def _():
            lax.fori_loop(0, length, column_strip, 0)

        if not last:
            return 0

        base = jnp.where(same, 0, r * MOST)
        ready = pl.ds(pl.multiple_of(base, MOST), MOST)
        lse[...] = tops[ready, :] + jnp.log2(totals[ready, :])
        mine = lse[pl.ds(own, 1), :]
        mine_up = upright(mine)

        def weigh(j, _):
            tile = kept[r, j]
            weight = jnp.exp2(tile - mine_up) + jnp.exp2(tile - lse[pl.ds(j, 1), :])
            weights[:, at(j)] = weight.astype(jnp.bfloat16)
            return 0

        def blank(j, _):
            weights[:, at(j)] = jnp.zeros((BLOCK, BLOCK), jnp.bfloat16)
            return 0

        lax.fori_loop(0, length, weigh, 0)
        lax.fori_loop(length, MOST, blank, 0)
        shift = shift_ref[pl.ds(r, 1), :]
        shift_up = upright(shift.astype(jnp.float32)).astype(jnp.int32)
        tile = kept[r, own]
        behind = row == jnp.bitwise_and(column + shift, BLOCK - 1)
        ahead = column == jnp.bitwise_and(row + shift_up, BLOCK - 1)
        weight = jnp.exp2(tile - mine_up) + jnp.exp2(tile - mine)
        weight = weight - jnp.where(ahead, 1.0, 0.0) - jnp.where(behind, 1.0, 0.0)
        weights[:, at(own)] = weight.astype(jnp.bfloat16)
        positive = jnp.sum(jnp.where(behind, tile, 0.0), axis=0, keepdims=True)
        loss_ref[pl.ds(r, 1), :] = (mine - positive) * (1.0 / log2e)
        total = jnp.dot(
            weights[...],
            window[pl.ds(pl.multiple_of(begin * BLOCK, BLOCK), span), :],
            preferred_element_type=jnp.float32,
        )
        grad_ref[at(r), :] = total * scale
        return 0

    lax.fori_loop(0, here, own_block, 0)


def run_stage(info, slabs, new_slots, prior_slots, state, shifts):
    rows, width = slabs[0].shape
    here = rows // BLOCK
    first, last = state is None, shifts is not None
    whole = pl.BlockSpec(memory_space=pltpu.VMEM)
    scalar = pl.BlockSpec(memory_space=pltpu.SMEM)
    state_shape = [
        pltpu.VMEM(((2 * REACH + 1) * rows, width), jnp.bfloat16),
        pltpu.VMEM((here, MOST, BLOCK, BLOCK), jnp.float32),
        pltpu.VMEM((here * MOST, BLOCK), jnp.float32),
        pltpu.VMEM((here * MOST, BLOCK), jnp.float32),
    ]
    args = [info, *slabs]
    in_specs = [scalar] + [pl.BlockSpec(memory_space=pl.ANY)] * len(slabs)
    out_shape, scratch = list(state_shape), []
    if last:
        args.append(shifts)
        in_specs.append(whole)
        out_shape = [
            jax.ShapeDtypeStruct((here, BLOCK), jnp.float32),
            jax.ShapeDtypeStruct((rows, width), jnp.float32),
        ] + out_shape
        scratch = [
            pltpu.VMEM((MOST, BLOCK), jnp.float32),
            pltpu.VMEM((BLOCK, MOST * BLOCK), jnp.bfloat16),
        ]
    aliases = {}
    if not first:
        aliases = {len(args) + n: len(out_shape) - len(state) + n for n in range(len(state))}
        args.extend(state)
        in_specs.extend([whole] * len(state))

    def body(*refs):
        stage(here, new_slots, prior_slots, first, last, refs)

    return pl.pallas_call(
        body,
        out_shape=tuple(out_shape),
        in_specs=in_specs,
        out_specs=tuple([whole] * len(out_shape)),
        scratch_shapes=[
            pltpu.VMEM((MOST * BLOCK, BLOCK), jnp.float32),
            pltpu.SemaphoreType.DMA((len(slabs),)),
        ]
        + scratch,
        input_output_aliases=aliases,
        compiler_params=pltpu.CompilerParams(vmem_limit_bytes=24 * 1024 * 1024),
        name="cluster_loss" if last else "cluster_scores",
    )(*args)


STAGES = ((0, 1, 2, 3, 4, 5), (6,), (7, 8, 9))


def cluster_extents(device, block_cluster, here):
    margin = jnp.full((REACH * here,), -1, jnp.int32)
    padded = jnp.concatenate([margin, block_cluster, margin])
    near = lax.dynamic_slice_in_dim(padded, device * here, (2 * REACH + 1) * here)
    info = [device]
    for own in (REACH * here, REACH * here + 1):
        mine = near == near[own]
        info.append(own - jnp.sum(mine[own - MOST + 1 : own]))
        info.append(own + 1 + jnp.sum(mine[own + 1 : own + MOST]))
    return jnp.stack(info + [device] * 3).astype(jnp.int32)


def local_work(info, shifts, slabs):
    rows = slabs[0].shape[0]
    state, prior = None, ()
    for new in STAGES[:-1]:
        state = run_stage(info, [slabs[n] for n in new], new, prior, state, None)
        prior = prior + new
    new = STAGES[-1]
    loss, grad, *_ = run_stage(info, [slabs[n] for n in new], new, prior, state, shifts)
    return loss.reshape(rows), grad


def shards(embeddings, block_cluster, partner_shift):
    here = embeddings.shape[0] // BLOCK
    device = lax.axis_index(AXES).astype(jnp.int32)
    info = cluster_extents(device, block_cluster, here)
    slabs, (info, shifts) = exchange(embeddings, info, partner_shift.reshape(here, BLOCK))
    return local_work(info, shifts, slabs)


def solution(mesh):
    in_specs = (P(AXES, None), P(), P(AXES))
    out_specs = (P(AXES), P(AXES, None))
    return jax.shard_map(shards, mesh=mesh, in_specs=in_specs, out_specs=out_specs, check_vma=False)
```

time: 156 us -> 76.6 us (0.49)
  the two profiles are of different devices: /device:TPU:233 before, /device:TPU:22 now
where the time goes in v3:
time: 76.6 us; the launch traced here: 75.2 us
  Pallas kernels  27.4 us (36%)
  starting transfers between devices  19.5 us (25%)
  waiting for transfers between devices  19 us (25%)
  between operations  3.23 us (4%)
  local copies, waits for them, and re-layouts  3.17 us (4%)
  other arithmetic  2.91 us (4%)
    pallas_call x3, Pallas kernels, run_stage(): pl.pallas_call(body, out_shape=tuple(out_shape), in_specs=in_specs, out_s...  27.4 us
    ppermute x9, starting transfers between devices, moved(): lax.ppermute(value, AXES, [(source, to % count) for source, to in pairs])  19.5 us
    ppermute x9, waiting for transfers between devices, moved(): lax.ppermute(value, AXES, [(source, to % count) for source, to in pairs])  19 us
    unnamed x3, local copies, waits for them, and re-layouts  1.71 us
  transfers between devices with their start and end apart: 9, of which 4 were waited for; matrix products, arithmetic and copies ran while one was open for 6% of the time, Pallas kernels for 22%

profile of v3, /device:TPU:22, one launch (start us, length us, event | category | flops | bytes accessed | tf_op | source)
XLA Modules:
  0.0 75.2 jit_solution(9596118225955515061)
XLA Ops:
  0.6 0.5 collective-permute-start.5
  1.2 1.4 %collective-permute-start = (bf16[512,768]{1,0:T(8,128)(2,1)}, bf16[512,768]{1,0:T(8,128)(2,1)S(1)}, u32[]{:S(2)}, u32[]{:S(2)}) collective-permute-start(bf16[512,768]{1,0:T(8,128)(2,1)} %refs_1_.1), channel_id=1, source_target_pairs={{0,252},{1,253},{2,254},{3,7},{4,0},{5,1},{6,2},{7,11},{8,4},{9,5}... | collective-permute-start | bytes 2359304 | tf_op jit(solution)/shard_map/ppermute | solution.py:23
  2.6 0.7 reshape.10.refs_4_
  3.3 0.8 %pad_add_fusion = s32[528]{0:T(1024)S(1)} fusion(s32[8]{0:T(128)S(1)} %broadcast.3, s32[512]{0:T(512)} %param.4), kind=kLoop, calls=%fused_computation | loop fusion | flops 1056 | bytes 4192 | tf_op jit(solution)/shard_map/concatenate | solution.py:282
  4.1 0.1 dynamic_slice.3
  4.1 0.6 fusion.4
  4.7 1.3 %broadcast_compare_fusion = (pred[18]{0:T(512)(128)(4,1)S(1)}, pred[18]{0:T(512)(128)(4,1)S(1)}) fusion(s32[]{:T(128)} %bitcast.4, s32[]{:T(128)} %bitcast.1, s32[528]{0:T(1024)S(1)} %pad_add_fusion, s32[]{:T(128)S(6)} %select_n.3), kind=kLoop, calls=%fused_computation.9 | loop fusion | flops 36 | bytes 120 | tf_op jit(solution)/shard_map/eq | solution.py:286
  6.1 0.8 %fusion.1 = (s32[]{:T(128)}, s32[]{:T(128)}, s32[]{:T(128)}, s32[]{:T(128)}) fusion(pred[18]{0:T(512)(128)(4,1)S(1)} %get-tuple-element.33, pred[18]{0:T(512)(128)(4,1)S(1)} %get-tuple-element.32), kind=kLoop, calls=%fused_computation.6 | loop fusion | flops 52 | bytes 44 | tf_op jit(solution)/shard_map/reduce_sum | solution.py:288
  9.4 3.5 %collective-permute-done.5.refs_5_ = bf16[512,768]{1,0:T(8,128)(2,1)S(1)} collective-permute-done((bf16[512,768]{1,0:T(8,128)(2,1)}, bf16[512,768]{1,0:T(8,128)(2,1)S(1)}, u32[]{:S(2)}, u32[]{:S(2)}) %collective-permute-start.5) | collective-permute-done | bytes 786464 | tf_op jit(solution)/shard_map/ppermute | solution.py:23
  12.9 2.5 %collective-permute-start.6 = (bf16[512,768]{1,0:T(8,128)(2,1)S(1)}, bf16[512,768]{1,0:T(8,128)(2,1)S(1)}, u32[]{:S(2)}, u32[]{:S(2)}) collective-permute-start(bf16[512,768]{1,0:T(8,128)(2,1)S(1)} %collective-permute-done.5.refs_5_), channel_id=1, source_target_pairs={{0,1},{1,0},{2,3},{3,2},{4,5},{5,4},{6,7},{7,6},{8,11},{9,10},{10,... | collective-permute-start | bytes 2359304 | tf_op jit(solution)/shard_map/ppermute | solution.py:23
  15.4 0.1 stack.26.refs_0_
  15.5 7.2 %collective-permute-done.refs_2_ = bf16[512,768]{1,0:T(8,128)(2,1)S(1)} collective-permute-done((bf16[512,768]{1,0:T(8,128)(2,1)}, bf16[512,768]{1,0:T(8,128)(2,1)S(1)}, u32[]{:S(2)}, u32[]{:S(2)}) %collective-permute-start) | collective-permute-done | bytes 786464 | tf_op jit(solution)/shard_map/ppermute | solution.py:23
  22.7 5.7 %collective-permute-start.8 = (bf16[512,768]{1,0:T(8,128)(2,1)}, bf16[512,768]{1,0:T(8,128)(2,1)S(1)}, u32[]{:S(2)}, u32[]{:S(2)}) collective-permute-start(bf16[512,768]{1,0:T(8,128)(2,1)} %refs_1_.1), channel_id=1, source_target_pairs={{0,1},{1,0},{2,3},{3,2},{4,5},{5,4},{6,7},{7,6},{8,11},{9,10},{10,... | collective-permute-start | bytes 2359304 | tf_op jit(solution)/shard_map/ppermute | solution.py:23
  28.4 2.3 %collective-permute-start.7 = (bf16[512,768]{1,0:T(8,128)(2,1)S(1)}, bf16[512,768]{1,0:T(8,128)(2,1)S(1)}, u32[]{:S(2)}, u32[]{:S(2)}) collective-permute-start(bf16[512,768]{1,0:T(8,128)(2,1)S(1)} %collective-permute-done.6.refs_4_), channel_id=1, source_target_pairs={{0,4},{1,5},{2,254},{3,255},{4,8},{5,9},{6,2},{7,3},{8,12},{9,13},... | collective-permute-start | bytes 2359304 | tf_op jit(solution)/shard_map/ppermute | solution.py:23
  30.7 1.3 %collective-permute-start.2 = (bf16[512,768]{1,0:T(8,128)(2,1)S(1)}, bf16[512,768]{1,0:T(8,128)(2,1)S(1)}, u32[]{:S(2)}, u32[]{:S(2)}) collective-permute-start(bf16[512,768]{1,0:T(8,128)(2,1)S(1)} %collective-permute-done.refs_2_), channel_id=1, source_target_pairs={{0,3},{3,2},{4,7},{7,6},{8,11},{11,10},{12,15},{15,14},{16,19},{19... | collective-permute-start | bytes 2359304 | tf_op jit(solution)/shard_map/ppermute | solution.py:23
  32.0 2.7 %collective-permute-start.1 = (bf16[512,768]{1,0:T(8,128)(2,1)S(1)}, bf16[512,768]{1,0:T(8,128)(2,1)S(1)}, u32[]{:S(2)}, u32[]{:S(2)}) collective-permute-start(bf16[512,768]{1,0:T(8,128)(2,1)S(1)} %collective-permute-done.refs_2_), channel_id=1, source_target_pairs={{0,1},{1,2},{2,3},{3,0},{4,5},{5,6},{6,7},{7,4},{8,9},{9,10},{10,1... | collective-permute-start | bytes 2359304 | tf_op jit(solution)/shard_map/ppermute | solution.py:23
  34.7 1.9 %collective-permute-done.3.refs_3_ = bf16[512,768]{1,0:T(8,128)(2,1)S(1)} collective-permute-done((bf16[512,768]{1,0:T(8,128)(2,1)S(1)}, bf16[512,768]{1,0:T(8,128)(2,1)S(1)}, u32[]{:S(2)}, u32[]{:S(2)}) %collective-permute-start.3) | collective-permute-done | bytes 786464 | tf_op jit(solution)/shard_map/ppermute | solution.py:23
  36.6 3.1 %collective-permute-start.4 = (bf16[512,768]{1,0:T(8,128)(2,1)S(1)}, bf16[512,768]{1,0:T(8,128)(2,1)S(1)}, u32[]{:S(2)}, u32[]{:S(2)}) collective-permute-start(bf16[512,768]{1,0:T(8,128)(2,1)S(1)} %collective-permute-done.3.refs_3_), channel_id=1, source_target_pairs={{1,0},{2,1},{5,4},{6,5},{9,8},{10,9},{13,12},{14,13},{17,16},{18,1... | collective-permute-start | bytes 2359304 | tf_op jit(solution)/shard_map/ppermute | solution.py:23
  39.7 6.4 %collective-permute-done.8.refs_6_ = bf16[512,768]{1,0:T(8,128)(2,1)S(1)} collective-permute-done((bf16[512,768]{1,0:T(8,128)(2,1)}, bf16[512,768]{1,0:T(8,128)(2,1)S(1)}, u32[]{:S(2)}, u32[]{:S(2)}) %collective-permute-start.8) | collective-permute-done | bytes 786464 | tf_op jit(solution)/shard_map/ppermute | solution.py:23
  46.1 1.1 %copy-done = bf16[512,768]{1,0:T(8,128)(2,1)S(1)} copy-done((bf16[512,768]{1,0:T(8,128)(2,1)S(1)}, bf16[512,768]{1,0:T(8,128)(2,1)}, u32[]{:S(2)}) %copy-start) | copy-done | bytes 786456
  47.2 11.1 %cluster_scores.2 = (bf16[4608,768]{1,0:T(8,128)(2,1)S(1)}, f32[2,8,256,256]{3,2,1,0:T(8,128)S(1)}, f32[16,256]{1,0:T(8,128)S(1)}, f32[16,256]{1,0:T(8,128)S(1)}) custom-call(s32[8]{0:T(128)S(1)} %stack.26.refs_0_, bf16[512,768]{1,0:T(8,128)(2,1)S(1)} %copy-done, bf16[512,768]{1,0:T(8,128)(2,1)S(1)} %collective-permute-done.refs_2_, ...), custom_call_target="tpu_custom_call" | custom-call | tf_op jit(solution)/shard_map/cluster_scores/pallas_call | solution.py:261
  58.3 5.3 %cluster_scores.3 = (bf16[4608,768]{1,0:T(8,128)(2,1)S(1)}, f32[2,8,256,256]{3,2,1,0:T(8,128)S(1)}, f32[16,256]{1,0:T(8,128)S(1)}, f32[16,256]{1,0:T(8,128)S(1)}) custom-call(s32[8]{0:T(128)S(1)} %stack.26.refs_0_, bf16[512,768]{1,0:T(8,128)(2,1)S(1)} %collective-permute-done.7.refs_1_, ...), custom_call_target="tpu_custom_call", output_to_operand_aliasing={{0}: (2, {}), {1}: (3, {}), {2}: (4, {}), {3}: (5, {})} | custom-call | tf_op jit(solution)/shard_map/cluster_scores/pallas_call | solution.py:261
  63.7 11.0 %cluster_loss.1 = (f32[2,256]{1,0:T(2,128)S(1)}, f32[512,768]{1,0:T(8,128)}, bf16[4608,768]{1,0:T(8,128)(2,1)S(1)}, f32[2,8,256,256]{3,2,1,0:T(8,128)S(1)}, f32[...) custom-call(s32[8]{0:T(128)S(1)} %stack.26.refs_0_, ...), custom_call_target="tpu_custom_call", output_to_operand_aliasing={{2}: (5, {}), {3}: (6, {}), {4}: (7, {}), {5}: (8, {})} | custom-call | tf_op jit(solution)/shard_map/cluster_loss/pallas_call | solution.py:261
  74.6 0.6 copy.13
  (8 shorter events, 0.0 us)
Async XLA Ops:
  0.6 12.3 %collective-permute-start.5 = (bf16[512,768]{1,0:T(8,128)(2,1)}, bf16[512,768]{1,0:T(8,128)(2,1)S(1)}, u32[]{:S(2)}, u32[]{:S(2)}) collective-permute-start(bf16[512,768]{1,0:T(8,128)(2,1)} %refs_1_.1), channel_id=1, source_target_pairs={{0,3},{1,2},{2,1},{3,0},{4,7},{5,6},{6,5},{7,4},{8,9},{9,8},{10,11... | collective-permute-start | bytes 2359304 | tf_op jit(solution)/shard_map/ppermute | solution.py:23
  1.2 21.6 %collective-permute-start = (bf16[512,768]{1,0:T(8,128)(2,1)}, bf16[512,768]{1,0:T(8,128)(2,1)S(1)}, u32[]{:S(2)}, u32[]{:S(2)}) collective-permute-start(bf16[512,768]{1,0:T(8,128)(2,1)} %refs_1_.1), channel_id=1, source_target_pairs={{0,252},{1,253},{2,254},{3,7},{4,0},{5,1},{6,2},{7,11},{8,4},{9,5}... | collective-permute-start | bytes 2359304 | tf_op jit(solution)/shard_map/ppermute | solution.py:23
  12.9 15.5 %collective-permute-start.6 = (bf16[512,768]{1,0:T(8,128)(2,1)S(1)}, bf16[512,768]{1,0:T(8,128)(2,1)S(1)}, u32[]{:S(2)}, u32[]{:S(2)}) collective-permute-start(bf16[512,768]{1,0:T(8,128)(2,1)S(1)} %collective-permute-done.5.refs_5_), channel_id=1, source_target_pairs={{0,1},{1,0},{2,3},{3,2},{4,5},{5,4},{6,7},{7,6},{8,11},{9,10},{10,... | collective-permute-start | bytes 2359304 | tf_op jit(solution)/shard_map/ppermute | solution.py:23
  22.7 13.9 %collective-permute-start.3 = (bf16[512,768]{1,0:T(8,128)(2,1)S(1)}, bf16[512,768]{1,0:T(8,128)(2,1)S(1)}, u32[]{:S(2)}, u32[]{:S(2)}) collective-permute-start(bf16[512,768]{1,0:T(8,128)(2,1)S(1)} %collective-permute-done.refs_2_), channel_id=1, source_target_pairs={{0,8},{1,9},{2,10},{3,251},{4,12},{5,13},{6,14},{7,255},{8,16},{9,... | collective-permute-start | bytes 2359304 | tf_op jit(solution)/shard_map/ppermute | solution.py:23
  22.7 23.3 %collective-permute-start.8 = (bf16[512,768]{1,0:T(8,128)(2,1)}, bf16[512,768]{1,0:T(8,128)(2,1)S(1)}, u32[]{:S(2)}, u32[]{:S(2)}) collective-permute-start(bf16[512,768]{1,0:T(8,128)(2,1)} %refs_1_.1), channel_id=1, source_target_pairs={{0,1},{1,0},{2,3},{3,2},{4,5},{5,4},{6,7},{7,6},{8,11},{9,10},{10,... | collective-permute-start | bytes 2359304 | tf_op jit(solution)/shard_map/ppermute | solution.py:23
  28.4 29.9 %collective-permute-start.7 = (bf16[512,768]{1,0:T(8,128)(2,1)S(1)}, bf16[512,768]{1,0:T(8,128)(2,1)S(1)}, u32[]{:S(2)}, u32[]{:S(2)}) collective-permute-start(bf16[512,768]{1,0:T(8,128)(2,1)S(1)} %collective-permute-done.6.refs_4_), channel_id=1, source_target_pairs={{0,4},{1,5},{2,254},{3,255},{4,8},{5,9},{6,2},{7,3},{8,12},{9,13},... | collective-permute-start | bytes 2359304 | tf_op jit(solution)/shard_map/ppermute | solution.py:23
  30.7 33.0 %collective-permute-start.2 = (bf16[512,768]{1,0:T(8,128)(2,1)S(1)}, bf16[512,768]{1,0:T(8,128)(2,1)S(1)}, u32[]{:S(2)}, u32[]{:S(2)}) collective-permute-start(bf16[512,768]{1,0:T(8,128)(2,1)S(1)} %collective-permute-done.refs_2_), channel_id=1, source_target_pairs={{0,3},{3,2},{4,7},{7,6},{8,11},{11,10},{12,15},{15,14},{16,19},{19... | collective-permute-start | bytes 2359304 | tf_op jit(solution)/shard_map/ppermute | solution.py:23
  32.0 31.7 %collective-permute-start.1 = (bf16[512,768]{1,0:T(8,128)(2,1)S(1)}, bf16[512,768]{1,0:T(8,128)(2,1)S(1)}, u32[]{:S(2)}, u32[]{:S(2)}) collective-permute-start(bf16[512,768]{1,0:T(8,128)(2,1)S(1)} %collective-permute-done.refs_2_), channel_id=1, source_target_pairs={{0,1},{1,2},{2,3},{3,0},{4,5},{5,6},{6,7},{7,4},{8,9},{9,10},{10,1... | collective-permute-start | bytes 2359304 | tf_op jit(solution)/shard_map/ppermute | solution.py:23
  36.6 27.1 %collective-permute-start.4 = (bf16[512,768]{1,0:T(8,128)(2,1)S(1)}, bf16[512,768]{1,0:T(8,128)(2,1)S(1)}, u32[]{:S(2)}, u32[]{:S(2)}) collective-permute-start(bf16[512,768]{1,0:T(8,128)(2,1)S(1)} %collective-permute-done.3.refs_3_), channel_id=1, source_target_pairs={{1,0},{2,1},{5,4},{6,5},{9,8},{10,9},{13,12},{14,13},{17,16},{18,1... | collective-permute-start | bytes 2359304 | tf_op jit(solution)/shard_map/ppermute | solution.py:23
  46.1 1.1 %copy-start = (bf16[512,768]{1,0:T(8,128)(2,1)S(1)}, bf16[512,768]{1,0:T(8,128)(2,1)}, u32[]{:S(2)}) copy-start(bf16[512,768]{1,0:T(8,128)(2,1)} %refs_1_.1) | copy-start | bytes 2359300
